TPU v7x, 32 devices: a whole 2x2x4 slice. The times are simulated.
32 devices in a mesh: seq: 16 (over z, y, core), head: 2 (over x).
Axes of the slice: x: 2, y: 2, z: 4, core: 2. Of those that a mesh axis runs over, the one named last changes fastest.
Arguments:
- tokens: bfloat16 [16384, 768], P(('seq', 'head')), may hold values from -6 to 6
- w_query: bfloat16 [768, 768], replicated, may hold values from -0.3125 to 0.3125
- w_key: bfloat16 [768, 768], replicated, may hold values from -0.21875 to 0.21875
- w_value: bfloat16 [768, 768], replicated, may hold values from -0.21875 to 0.21875
- w_out: bfloat16 [768, 768], replicated, may hold values from -3.5 to 3.5
- gain_attn: float32 [768], replicated, may hold values from 0.5 to 1.5
- shift_attn: float32 [768], replicated, may hold values from -3 to 3
- w_up: bfloat16 [768, 3072], replicated, may hold values from -0.21875 to 0.21875
- w_down: bfloat16 [3072, 768], replicated, may hold values from -0.109375 to 0.109375
- gain_mlp: float32 [768], replicated, may hold values from 0.5 to 1.5
- shift_mlp: float32 [768], replicated, may hold values from -3 to 3
- cotangent: bfloat16 [16384, 768], P(('seq', 'head')), may hold values from -6 to 6
- lengths: int32 [8], replicated, may hold values from 1 to 64, 256 in all
- seq_order: int32 [8], replicated, may hold values from 0 to 7, each once
- rand_blocks: int32 [256, 3], P('seq'), may hold values from 0 to 65535
Outputs:
- output: bfloat16 [16384, 768], P(('seq', 'head'))
- grad_tokens: float32 [16384, 768], P(('seq', 'head'))
- grad_w_query: float32 [768, 768], P('seq')
- grad_w_key: float32 [768, 768], P('seq')
- grad_w_value: float32 [768, 768], P('seq')
- grad_w_out: float32 [768, 768], P('seq')
- grad_gain_attn: float32 [768], P('seq')
- grad_shift_attn: float32 [768], P('seq')
- grad_w_up: float32 [768, 3072], P('seq')
- grad_w_down: float32 [3072, 768], P('seq')
- grad_gain_mlp: float32 [768], P('seq')
- grad_shift_mlp: float32 [768], P('seq')
Inputs may be any that keep to these rules, and one draw needn't show every extreme that they name: lengths of the 8 sequences in blocks of 64 tokens; they sum to 256 and the longest is exactly 64. `seq_order`: each of 0 to 7 once.
All inputs are finite; a program needn't handle non-finite values.
Results may differ from a plain program's by a relative error of at most 0.017.
Values may be sent and summed in bfloat16 or wider, within the bound.
A program may use at most 320 MiB of HBM per device.

v0:
```python
import jax
import jax.numpy as jnp
from jax import lax
from jax.sharding import PartitionSpec as P

DH = 64
BLK = 64
MAXB = 64


eps_norm = 1e-06


def shifted(value, axis, steps):
    count = lax.axis_size(axis)
    first, last = (max(0, -steps), min(count, count - steps))
    return lax.ppermute(value, axis, [(source, source + steps) for source in range(first, last)])


def block_slots(blocks, rand_rows, lengths, seq_order):
    seq_count = lengths.shape[0]
    seq_ids = jnp.arange(seq_count, dtype=jnp.int32)
    packed = jnp.sum(jnp.where(seq_order[:, None] == seq_ids[None, :], lengths[None, :], 0), axis=1)
    seq_ends = jnp.cumsum(packed)
    starts = seq_ends - packed
    holder = jnp.sum((seq_ends[None, :] <= blocks[:, None]).astype(jnp.int32), axis=1)
    chosen = holder[:, None] == seq_ids[None, :]
    seq_first = jnp.sum(jnp.where(chosen, starts[None, :], 0), axis=1)
    seq_span = jnp.sum(jnp.where(chosen, packed[None, :], 0), axis=1)
    offset = blocks - seq_first
    rand_pos = seq_first[:, None] + jnp.mod(rand_rows, seq_span[:, None])
    fixed_cand = jnp.stack(
        [blocks - 1, blocks, blocks + 1, seq_first, seq_first + seq_span - 1], axis=1
    )
    candidate = jnp.concatenate([fixed_cand, rand_pos], axis=1)
    fixed_live = jnp.stack(
        [offset > 0, offset >= 0, offset < seq_span - 1, offset >= 0, offset >= 0], axis=1
    )
    usable = jnp.concatenate([fixed_live, rand_pos >= 0], axis=1)
    kept_list = []
    for column in range(candidate.shape[1]):
        unique = usable[:, column]
        for earlier in range(column):
            unique = unique & jnp.logical_not(
                kept_list[earlier] & (candidate[:, earlier] == candidate[:, column])
            )
        kept_list.append(unique)
    is_live = jnp.stack(kept_list, axis=1)
    key_blocks = jnp.where(is_live, candidate, blocks[:, None])
    return (key_blocks, is_live)


def norm_forward(values, gain_vec, shift_vec):
    center = values - jnp.mean(values, axis=-1, keepdims=True)
    spread = jnp.mean(center * center, axis=-1, keepdims=True)
    inv_dev = lax.rsqrt(spread + eps_norm)
    x_hat = center * inv_dev
    return (x_hat * gain_vec + shift_vec, x_hat, inv_dev)


def norm_backward(grad_in, x_hat, inv_dev, gain_vec):
    grad_gain = jnp.sum(grad_in * x_hat, axis=0)
    grad_shift = jnp.sum(grad_in, axis=0)
    grad_hat = grad_in * gain_vec
    grad_mean = jnp.mean(grad_hat, axis=-1, keepdims=True)
    grad_proj = jnp.mean(grad_hat * x_hat, axis=-1, keepdims=True)
    return (inv_dev * (grad_hat - grad_mean - x_hat * grad_proj), grad_gain, grad_shift)


def gelu_tanh(values):
    return jax.nn.gelu(values, approximate=True)


def kv_from_below(piece):
    return shifted(piece, "seq", 1)


def kv_from_above(piece):
    return shifted(piece, "seq", -1)


def kv_again_below(piece):
    return shifted(piece, "seq", 1)


def kv_again_above(piece):
    return shifted(piece, "seq", -1)


def fill_cycle(kv_local, cycle_reach, from_below, from_above):
    slot_total = 2 * cycle_reach + 1
    buffer = jnp.zeros((slot_total,) + kv_local.shape, kv_local.dtype)
    buffer = lax.dynamic_update_index_in_dim(buffer, kv_local, cycle_reach, 0)

    def advance(cycle_step, cycle_state):
        below_piece, above_piece, filled = cycle_state
        below_piece = from_below(below_piece)
        above_piece = from_above(above_piece)
        filled = lax.dynamic_update_index_in_dim(
            filled, below_piece, cycle_reach - cycle_step - 1, 0
        )
        filled = lax.dynamic_update_index_in_dim(
            filled, above_piece, cycle_reach + cycle_step + 1, 0
        )
        return (below_piece, above_piece, filled)

    return lax.fori_loop(0, cycle_reach, advance, (kv_local, kv_local, buffer))[2]


def gather_slots(buffer, local_rows, heads_here):
    flat_rows = buffer.reshape(-1, BLK, buffer.shape[-1])
    picked = flat_rows[local_rows]
    split_shape = picked.shape[:3] + (2, heads_here, DH)
    picked = picked.reshape(split_shape)
    return (picked[:, :, :, 0], picked[:, :, :, 1])


def score_blocks(q_blocks, key_rows, is_live, score_scale):
    scores = (
        jnp.einsum("cqhd,cskhd->chqsk", q_blocks, key_rows, preferred_element_type=jnp.float32)
        * score_scale
    )
    scores = jnp.where(is_live[:, None, None, :, None], scores, -1e30)
    return scores.reshape(scores.shape[0], scores.shape[1], scores.shape[2], -1)


def body(
    tokens,
    w_query,
    w_key,
    w_value,
    w_out,
    gain_attn,
    shift_attn,
    w_up,
    w_down,
    gain_mlp,
    shift_mlp,
    cotangent,
    lengths,
    seq_order,
    rand_blocks,
):
    score_scale = DH ** (-0.5)
    queries = jnp.dot(tokens, w_query, preferred_element_type=jnp.float32).astype(jnp.bfloat16)
    key_proj = jnp.dot(tokens, w_key, preferred_element_type=jnp.float32).astype(jnp.bfloat16)
    value_proj = jnp.dot(tokens, w_value, preferred_element_type=jnp.float32).astype(jnp.bfloat16)
    q_local, k_local, v_local = (
        lax.all_to_all(queries, "head", split_axis=1, concat_axis=0, tiled=True),
        lax.all_to_all(key_proj, "head", split_axis=1, concat_axis=0, tiled=True),
        lax.all_to_all(value_proj, "head", split_axis=1, concat_axis=0, tiled=True),
    )
    stretch_rows = q_local.shape[0]
    heads_here = q_local.shape[1] // DH
    stretch_blocks = stretch_rows // BLK
    cycle_reach = MAXB * BLK // stretch_rows
    kv_local = jnp.concatenate([k_local, v_local], axis=1)
    buffer = fill_cycle(kv_local, cycle_reach, kv_from_below, kv_from_above)
    seq_index = lax.axis_index("seq")
    blocks = seq_index * stretch_blocks + jnp.arange(stretch_blocks, dtype=jnp.int32)
    key_blocks, is_live = block_slots(blocks, rand_blocks, lengths, seq_order)
    local_rows = key_blocks - (seq_index - cycle_reach) * stretch_blocks
    slot_count = key_blocks.shape[1]
    q_blocks = q_local.reshape(stretch_blocks, BLK, heads_here, DH)
    key_rows, value_rows = gather_slots(buffer, local_rows, heads_here)
    scores = score_blocks(q_blocks, key_rows, is_live, score_scale)
    row_max = jnp.max(scores, axis=-1, keepdims=True)
    exp_scores = jnp.exp(scores - row_max)
    row_total = jnp.sum(exp_scores, axis=-1, keepdims=True)
    attn_probs = exp_scores / row_total
    log_total = row_max + jnp.log(row_total)
    five_shape = (stretch_blocks, heads_here, BLK, slot_count, BLK)
    weights = attn_probs.astype(jnp.bfloat16).reshape(five_shape)
    context = jnp.einsum(
        "chqsk,cskhd->cqhd", weights, value_rows, preferred_element_type=jnp.float32
    )
    context = context.astype(jnp.bfloat16).reshape(stretch_rows, -1)
    context_tok = lax.all_to_all(context, "head", split_axis=0, concat_axis=1, tiled=True)
    attn_out = jnp.dot(context_tok, w_out, preferred_element_type=jnp.float32)
    normed, hat_one, dev_one = norm_forward(
        tokens.astype(jnp.float32) + attn_out, gain_attn, shift_attn
    )
    normed_low = normed.astype(jnp.bfloat16)
    hidden_pre = jnp.dot(normed_low, w_up, preferred_element_type=jnp.float32)
    hidden = gelu_tanh(hidden_pre).astype(jnp.bfloat16)
    mlp_out = jnp.dot(hidden, w_down, preferred_element_type=jnp.float32)
    output, hat_two, dev_two = norm_forward(normed + mlp_out, gain_mlp, shift_mlp)
    grad_two, grad_gain_mlp, grad_shift_mlp = norm_backward(
        cotangent.astype(jnp.float32), hat_two, dev_two, gain_mlp
    )
    grad_mlp = grad_two.astype(jnp.bfloat16)
    grad_w_down = jnp.dot(hidden.T, grad_mlp, preferred_element_type=jnp.float32)
    grad_hidden = jnp.dot(grad_mlp, w_down.T, preferred_element_type=jnp.float32)
    gelu_out, gelu_pull = jax.vjp(gelu_tanh, hidden_pre)
    grad_pre = gelu_pull(grad_hidden)[0].astype(jnp.bfloat16)
    grad_w_up = jnp.dot(normed_low.T, grad_pre, preferred_element_type=jnp.float32)
    grad_normed = grad_two + jnp.dot(grad_pre, w_up.T, preferred_element_type=jnp.float32)
    grad_one, grad_gain_attn, grad_shift_attn = norm_backward(
        grad_normed, hat_one, dev_one, gain_attn
    )
    grad_attn = grad_one.astype(jnp.bfloat16)
    grad_w_out = jnp.dot(context_tok.T, grad_attn, preferred_element_type=jnp.float32)
    grad_context = jnp.dot(grad_attn, w_out.T, preferred_element_type=jnp.float32).astype(
        jnp.bfloat16
    )
    grad_ctx_local = lax.all_to_all(grad_context, "head", split_axis=1, concat_axis=0, tiled=True)
    buffer_back = fill_cycle(kv_local, cycle_reach, kv_again_below, kv_again_above)
    key_again, value_again = gather_slots(buffer_back, local_rows, heads_here)
    scores_again = score_blocks(q_blocks, key_again, is_live, score_scale)
    probs_again = jnp.exp(scores_again - log_total)
    weights_again = probs_again.astype(jnp.bfloat16).reshape(five_shape)
    grad_blocks = grad_ctx_local.reshape(stretch_blocks, BLK, heads_here, DH)
    grad_probs = jnp.einsum(
        "cqhd,cskhd->chqsk", grad_blocks, value_again, preferred_element_type=jnp.float32
    )
    grad_probs = grad_probs.reshape(probs_again.shape)
    grad_value_rows = jnp.einsum(
        "chqsk,cqhd->cskhd", weights_again, grad_blocks, preferred_element_type=jnp.float32
    )
    row_inner = jnp.sum(probs_again * grad_probs, axis=-1, keepdims=True)
    grad_scores = (probs_again * (grad_probs - row_inner)).astype(jnp.bfloat16).reshape(five_shape)
    grad_query = (
        jnp.einsum("chqsk,cskhd->cqhd", grad_scores, key_again, preferred_element_type=jnp.float32)
        * score_scale
    )
    grad_key_rows = (
        jnp.einsum("chqsk,cqhd->cskhd", grad_scores, q_blocks, preferred_element_type=jnp.float32)
        * score_scale
    )
    slot_grads = jnp.concatenate(
        [
            grad_key_rows.reshape(stretch_blocks, slot_count, BLK, -1),
            grad_value_rows.reshape(stretch_blocks, slot_count, BLK, -1),
        ],
        axis=-1,
    )
    width_kv = slot_grads.shape[-1]
    grad_buffer = jnp.zeros((buffer.shape[0] * stretch_blocks, BLK, width_kv), jnp.float32)
    grad_buffer = grad_buffer.at[local_rows.reshape(-1)].add(slot_grads.reshape(-1, BLK, width_kv))
    grad_buffer = grad_buffer.reshape(buffer.shape[0], stretch_rows, width_kv)

    def carry_back(cycle_step, cycle_state):
        below_acc, above_acc = cycle_state
        below_term = lax.dynamic_index_in_dim(grad_buffer, cycle_step, 0, keepdims=False)
        above_term = lax.dynamic_index_in_dim(
            grad_buffer, 2 * cycle_reach - cycle_step, 0, keepdims=False
        )
        below_acc = shifted((below_acc + below_term).astype(jnp.bfloat16), "seq", -1).astype(
            jnp.float32
        )
        above_acc = shifted((above_acc + above_term).astype(jnp.bfloat16), "seq", 1).astype(
            jnp.float32
        )
        return (below_acc, above_acc)

    zero_rows = jnp.zeros((stretch_rows, width_kv), jnp.float32)
    below_acc, above_acc = lax.fori_loop(0, cycle_reach, carry_back, (zero_rows, zero_rows))
    grad_kv = below_acc + above_acc + grad_buffer[cycle_reach]
    half_width = width_kv // 2
    grad_key_local = grad_kv[:, :half_width].astype(jnp.bfloat16)
    grad_value_local = grad_kv[:, half_width:].astype(jnp.bfloat16)
    grad_query_local = grad_query.reshape(stretch_rows, -1).astype(jnp.bfloat16)
    grad_q_tok, grad_k_tok, grad_v_tok = (
        lax.all_to_all(grad_query_local, "head", split_axis=0, concat_axis=1, tiled=True),
        lax.all_to_all(grad_key_local, "head", split_axis=0, concat_axis=1, tiled=True),
        lax.all_to_all(grad_value_local, "head", split_axis=0, concat_axis=1, tiled=True),
    )
    grad_w_query = jnp.dot(tokens.T, grad_q_tok, preferred_element_type=jnp.float32)
    grad_w_key = jnp.dot(tokens.T, grad_k_tok, preferred_element_type=jnp.float32)
    grad_w_value = jnp.dot(tokens.T, grad_v_tok, preferred_element_type=jnp.float32)
    grad_tokens = grad_one + jnp.dot(grad_q_tok, w_query.T, preferred_element_type=jnp.float32)
    grad_tokens = grad_tokens + jnp.dot(grad_k_tok, w_key.T, preferred_element_type=jnp.float32)
    grad_tokens = grad_tokens + jnp.dot(grad_v_tok, w_value.T, preferred_element_type=jnp.float32)
    grad_terms = (
        grad_w_query,
        grad_w_key,
        grad_w_value,
        grad_w_out,
        grad_gain_attn,
        grad_shift_attn,
        grad_w_up,
        grad_w_down,
        grad_gain_mlp,
        grad_shift_mlp,
    )
    shares = (
        lax.psum_scatter(grad_terms[0], "seq", scatter_dimension=0, tiled=True),
        lax.psum_scatter(grad_terms[1], "seq", scatter_dimension=0, tiled=True),
        lax.psum_scatter(grad_terms[2], "seq", scatter_dimension=0, tiled=True),
        lax.psum_scatter(grad_terms[3], "seq", scatter_dimension=0, tiled=True),
        lax.psum_scatter(grad_terms[4], "seq", scatter_dimension=0, tiled=True),
        lax.psum_scatter(grad_terms[5], "seq", scatter_dimension=0, tiled=True),
        lax.psum_scatter(grad_terms[6], "seq", scatter_dimension=0, tiled=True),
        lax.psum_scatter(grad_terms[7], "seq", scatter_dimension=0, tiled=True),
        lax.psum_scatter(grad_terms[8], "seq", scatter_dimension=0, tiled=True),
        lax.psum_scatter(grad_terms[9], "seq", scatter_dimension=0, tiled=True),
    )
    totals = (
        lax.psum(shares[0].astype(jnp.bfloat16), "head").astype(jnp.float32),
        lax.psum(shares[1].astype(jnp.bfloat16), "head").astype(jnp.float32),
        lax.psum(shares[2].astype(jnp.bfloat16), "head").astype(jnp.float32),
        lax.psum(shares[3].astype(jnp.bfloat16), "head").astype(jnp.float32),
        lax.psum(shares[4].astype(jnp.bfloat16), "head").astype(jnp.float32),
        lax.psum(shares[5].astype(jnp.bfloat16), "head").astype(jnp.float32),
        lax.psum(shares[6].astype(jnp.bfloat16), "head").astype(jnp.float32),
        lax.psum(shares[7].astype(jnp.bfloat16), "head").astype(jnp.float32),
        lax.psum(shares[8].astype(jnp.bfloat16), "head").astype(jnp.float32),
        lax.psum(shares[9].astype(jnp.bfloat16), "head").astype(jnp.float32),
    )
    return (
        output.astype(jnp.bfloat16),
        grad_tokens,
        totals[0],
        totals[1],
        totals[2],
        totals[3],
        totals[4],
        totals[5],
        totals[6],
        totals[7],
        totals[8],
        totals[9],
    )


def solution(mesh):
    return jax.shard_map(
        body,
        mesh=mesh,
        in_specs=(
            P(("seq", "head"), None),
            P(),
            P(),
            P(),
            P(),
            P(),
            P(),
            P(),
            P(),
            P(),
            P(),
            P(("seq", "head"), None),
            P(),
            P(),
            P("seq", None),
        ),
        out_specs=(
            P(("seq", "head"), None),
            P(("seq", "head"), None),
            P("seq", None),
            P("seq", None),
            P("seq", None),
            P("seq", None),
            P("seq"),
            P("seq"),
            P("seq", None),
            P("seq", None),
            P("seq"),
            P("seq"),
        ),
        check_vma=False,
    )
```

profile of v0, /device:TPU:24, one launch (start us, length us, event | category | flops | bytes accessed | tf_op | source)
XLA Modules:
  0.0 1418.6 jit_solution(9601776251737171842)
XLA Ops:
  53.5 184.0 %while.42 = (s32[]{:T(128)}, bf16[1024,768]{1,0:T(8,128)(2,1)}, bf16[1024,768]{1,0:T(8,128)(2,1)}, bf16[9,1024,768]{2,1,0:T(8,128)(2,1)}, s32[]{:T(128)}, /*inde...) while((s32[]{:T(128)}, bf16[1024,768]{1,0:T(8,128)(2,1)}, bf16[1024,768]{1,0:T(8,128)(2,1)}, ...), condition=%wide.region_1.2_spmd, body=%wide.region_0.1_spmd.sunk | while | flops 10 | bytes 25166100 | solution.py:107
  84.8 33.6 %collective-permute-start = (bf16[1024,768]{1,0:T(8,128)(2,1)}, bf16[1024,768]{1,0:T(8,128)(2,1)S(1)}, u32[]{:S(2)}, u32[]{:S(2)}) collective-permute-start(bf16[1024,768]{1,0:T(8,128)(2,1)} %get-tuple-element.438), channel_id=1, source_target_pairs={{0,2},{2,4},{4,6},{6,8},{8,10},{10,12},{12,14},{14,16},{16,18},{18... | collective-permute-start | bytes 4718600 | tf_op jit(solution)/shard_map/while/body/eval_jaxpr/ppermute | solution.py:17
  176.9 33.6 %collective-permute-start = (bf16[1024,768]{1,0:T(8,128)(2,1)}, bf16[1024,768]{1,0:T(8,128)(2,1)S(1)}, u32[]{:S(2)}, u32[]{:S(2)}) collective-permute-start(bf16[1024,768]{1,0:T(8,128)(2,1)} %get-tuple-element.438), channel_id=1, source_target_pairs={{0,2},{2,4},{4,6},{6,8},{8,10},{10,12},{12,14},{14,16},{16,18},{18... | collective-permute-start | bytes 4718600 | tf_op jit(solution)/shard_map/while/body/eval_jaxpr/ppermute | solution.py:17
  250.7 38.9 %reshape.689 = bf16[16,8,64,2,6,64]{5,4,3,2,1,0:T(8,128)(2,1)} reshape(bf16[128,64,768]{2,1,0:T(8,128)(2,1)} %gather_fusion) | data formatting | bytes 25165824 | tf_op jit(solution)/shard_map/reshape | solution.py:114
  289.6 28.4 %slice_bitcast_fusion = (bf16[16,8,64,6,64]{4,3,2,1,0:T(8,128)(2,1)}, bf16[16,8,64,1,6,64]{5,4,3,2,1,0:T(8,128)(2,1)}, bf16[16,8,64,1,6,64]{5,4,3,2,1,0:T(8,128)(2,1)}) fusion(bf16[16,8,64,2,6,64]{5,4,3,2,1,0:T(8,128)(2,1)} %reshape.689), kind=kLoop, calls=%fused_computation.149 | loop fusion | bytes 31457280 | tf_op jit(solution)/shard_map/squeeze | solution.py:115
  332.3 22.2 %copy.221 = bf16[16,8,64,1,6,64]{2,5,1,4,0,3:T(8,128)(2,1)} copy(bf16[16,8,64,1,6,64]{5,4,3,2,1,0:T(8,128)(2,1)} %get-tuple-element.343) | data formatting | bytes 12582912
  464.6 24.5 %multiply_reduce_fusion = (f32[16,6,64]{2,1,0:T(8,128)S(1)}, f32[16,6,64,512]{2,3,1,0}) fusion(f32[16,6,64]{2,1,0:T(8,128)S(1)} %log_add_fusion, pred[16,8]{1,0:T(8,128)(4,1)S(1)} %copy.170, f32[16,6,64,512]{2,3,1,0} %get-tuple-element.361, bf16[16,6,64,512]{2,3,1,0:T(8,128)(2,1)} %bitcast.275, bf16[16,64,6,64]{1,0,3,2:T(8,128)(2,1)S(1)} %reshape.691), kind=kOutput, calls=%fused_computation.11 | convolution fusion | flops 418375680 | bytes 32292992
  489.1 21.9 %multiply_convert_fusion = bf16[16,6,64,8,64]{2,4,3,1,0:T(8,128)(2,1)} fusion(f32[16,6,64]{2,1,0:T(8,128)S(1)} %get-tuple-element.367, f32[16,6,64]{2,1,0:T(8,128)S(1)} %log_add_fusion, pred[16,8]{1,0:T(8,128)(4,1)S(1)} %copy.170, f32[16,6,64,512]{2,3,1,0} %get-tuple-element.368, f32[16,6,64,512]{2,3,1,0} %get-tuple-element.361), kind=kLoop, calls=%fused_computation.10 | loop fusion | flops 18874368 | bytes 31506560 | tf_op jit(solution)/shard_map/convert_element_type | solution.py:221
  531.6 24.7 %fusion.12 = f32[16,8,64,6,64]{2,4,1,3,0:T(8,128)} fusion(f32[16,6,64]{2,1,0:T(8,128)S(1)} %log_add_fusion, f32[16,6,64,8,64]{2,4,3,1,0:T(8,128)} %bitcast.271, pred[16,8]{1,0:T(8,128)(4,1)S(1)} %copy.170, bf16[16,64,6,64,1]{1,0,3,2,4:T(8,128)(2,1)S(1)} %bitcast.277), kind=kOutput, calls=%fused_computation.27 | convolution fusion | flops 415236096 | bytes 25976960 | tf_op jit(solution)/shard_map/chqsk,cqhd->cskhd/dot_general | solution.py:217
  569.1 29.1 %copy.190 = f32[16,8,64,6,64]{4,3,2,1,0:T(8,128)} copy(f32[16,8,64,6,64]{4,2,1,3,0:T(8,128)} %multiply_bitcast_fusion) | data formatting | bytes 25165824 | tf_op jit(solution)/shard_map/mul | solution.py:227
  598.2 25.1 %concatenate.51 = f32[128,64,384]{2,1,0:T(8,128)} reshape(f32[16,8,64,6,64]{4,3,2,1,0:T(8,128)} %copy.190) | data formatting | bytes 25165824 | tf_op jit(solution)/shard_map/concatenate | solution.py:230
  623.3 28.8 %copy.193 = f32[16,8,64,6,64]{4,3,2,1,0:T(8,128)} copy(f32[16,8,64,6,64]{2,4,1,3,0:T(8,128)} %fusion.12) | data formatting | bytes 25165824 | tf_op jit(solution)/shard_map/chqsk,cqhd->cskhd/transpose | solution.py:217
  652.1 25.2 %concatenate.52 = f32[128,64,384]{2,1,0:T(8,128)} reshape(f32[16,8,64,6,64]{4,3,2,1,0:T(8,128)} %copy.193) | data formatting | bytes 25165824 | tf_op jit(solution)/shard_map/concatenate | solution.py:230
  682.1 17.8 %pad_maximum_fusion = f32[128,64,768]{2,1,0:T(8,128)} fusion(f32[128,64,384]{2,1,0:T(8,128)} %concatenate.52, f32[128,64,384]{2,1,0:T(8,128)} %concatenate.51), kind=kLoop, calls=%fused_computation.8 | loop fusion | flops 6291456 | bytes 50331648 | tf_op jit(solution)/shard_map/concatenate | solution.py:230
  713.0 63.8 %scatter_fusion = f32[144,64,768]{2,1,0:T(8,128)} fusion(f32[144,64,768]{2,1,0:T(8,128)} %broadcast_in_dim.126, s32[128]{0:T(128)S(1)} %copy-done.63, f32[128,64,768]{2,1,0:T(8,128)} %pad_maximum_fusion), kind=kCustom, calls=%fused_computation.1 | custom fusion | flops 6291456 | bytes 75497984 | tf_op jit(solution)/shard_map/scatter-add | solution.py:239
  780.7 171.7 %while.43 = (s32[]{:T(128)}, f32[1024,768]{1,0:T(8,128)}, f32[1024,768]{1,0:T(8,128)}, f32[9,1024,768]{2,1,0:T(8,128)}, s32[]{:T(128)}, /*index=5*/s32[]{:T(128)}, s32[]{:T(128)}, s32[]{:T(128)}) while((s32[]{:T(128)}, f32[1024,768]{1,0:T(8,128)}, f32[1024,768]{1,0:T(8,128)}, f32[9,1024,768]{2,1,0:T(8,128)}, s32[]{:T(128)}, ...), condition=%wide.region_20.21_spmd.clone, body=%wide.region_19.20_spmd.clone.sunk | while | flops 6291463 | bytes 37748964 | solution.py:257
  824.1 18.3 %collective-permute-start.3 = (bf16[1024,768]{1,0:T(8,128)(2,1)S(1)}, bf16[1024,768]{1,0:T(8,128)(2,1)}, u32[]{:S(2)}, u32[]{:S(2)}) collective-permute-start(bf16[1024,768]{1,0:T(8,128)(2,1)S(1)} %get-tuple-element.426), channel_id=1, source_target_pairs={{0,2},{2,4},{4,6},{6,8},{8,10},{10,12},{12,14},{14,16},{16,18},{18... | collective-permute-start | bytes 4718600 | tf_op jit(solution)/shard_map/while/body/eval_jaxpr/ppermute | solution.py:17
  874.4 20.2 %collective-permute-start.3 = (bf16[1024,768]{1,0:T(8,128)(2,1)S(1)}, bf16[1024,768]{1,0:T(8,128)(2,1)}, u32[]{:S(2)}, u32[]{:S(2)}) collective-permute-start(bf16[1024,768]{1,0:T(8,128)(2,1)S(1)} %get-tuple-element.426), channel_id=1, source_target_pairs={{0,2},{2,4},{4,6},{6,8},{8,10},{10,12},{12,14},{14,16},{16,18},{18... | collective-permute-start | bytes 4718600 | tf_op jit(solution)/shard_map/while/body/eval_jaxpr/ppermute | solution.py:17
  922.7 21.8 %collective-permute-start.3 = (bf16[1024,768]{1,0:T(8,128)(2,1)S(1)}, bf16[1024,768]{1,0:T(8,128)(2,1)}, u32[]{:S(2)}, u32[]{:S(2)}) collective-permute-start(bf16[1024,768]{1,0:T(8,128)(2,1)S(1)} %get-tuple-element.426), channel_id=1, source_target_pairs={{0,2},{2,4},{4,6},{6,8},{8,10},{10,12},{12,14},{14,16},{16,18},{18... | collective-permute-start | bytes 4718600 | tf_op jit(solution)/shard_map/while/body/eval_jaxpr/ppermute | solution.py:17
  1014.8 64.5 %all-reduce.5 = (bf16[768]{0:T(1024)(128)(2,1)S(1)}, bf16[768]{0:T(1024)(128)(2,1)S(1)}, bf16[768]{0:T(1024)(128)(2,1)S(1)}, bf16[768]{0:T(1024)(128)(2,1)S(1)}) all-reduce(f32[768]{0:T(1024)S(1)} %copy-done.49, f32[768]{0:T(1024)S(1)} %copy-done.50, f32[768]{0:T(1024)S(1)} %copy-done.29, ...), channel_id=6, replica_groups=mesh['seq'=16,'head'=2] {'seq'}, use_global_device_ids=true, to_apply=%region_30.31.clone | all-reduce | flops 3072 | bytes 18432
  1091.5 29.5 %reduce-scatter.23.cloned.1.call-done = f32[48,768]{1,0:T(8,128)} async-done(((f32[768,768]{1,0:T(8,128)}), f32[48,768]{1,0:T(8,128)}) %reduce-scatter.23.cloned.1.call-update) | async-done | bytes 147472
  1122.8 112.6 %reduce-scatter.17.cloned.1.call-done = f32[192,768]{1,0:T(8,128)} async-done(((f32[3072,768]{1,0:T(8,128)}), f32[192,768]{1,0:T(8,128)}) %reduce-scatter.17.cloned.1.call-update) | async-done | bytes 589840 | tf_op jit(solution)/shard_map/reduce_scatter | solution.py:294
  1237.2 113.8 %reduce-scatter.15.cloned.1.call-done = f32[48,3072]{1,0:T(8,128)} async-done(((f32[768,3072]{1,0:T(8,128)}), f32[48,3072]{1,0:T(8,128)}) %reduce-scatter.15.cloned.1.call-update) | async-done | bytes 589840 | tf_op jit(solution)/shard_map/reduce_scatter | solution.py:293
  1358.1 43.1 %all-reduce.10.cloned.1.call-done = (bf16[48,768]{0,1:T(8,128)(2,1)}, bf16[48,768]{0,1:T(8,128)(2,1)}, bf16[48,768]{0,1:T(8,128)(2,1)}, bf16[48,768]{1,0:T(8,128...) async-done(((bf16[48,768]{0,1:T(8,128)(2,1)}, bf16[48,768]{0,1:T(8,128)(2,1)}, bf16[48,768]{0,1:T(8,128)(2,1)}, bf16[48,768]{1,0:T(8,128)(2,1)}, ...) | async-done | bytes 884752 | tf_op jit(solution)/shard_map/psum | solution.py:299
  (356 shorter events, 560.7 us)
Async XLA Ops:
  39.1 290.2 %all-to-all-start.2 = ((bf16[512,2,384]{0,2,1:T(8,128)(2,1)}), bf16[512,2,384]{0,2,1:T(8,128)(2,1)}, u32[]{:S(2)}, u32[]{:S(2)}) async-start(bf16[512,2,384]{0,2,1:T(8,128)(2,1)} %bitcast.40), calls=%async_computation.2 | async-start | bytes 1572864 | tf_op jit(solution)/shard_map/all_to_all | solution.py:149
  53.5 22.9 %collective-permute-start = (bf16[1024,768]{1,0:T(8,128)(2,1)}, bf16[1024,768]{1,0:T(8,128)(2,1)S(1)}, u32[]{:S(2)}, u32[]{:S(2)}) collective-permute-start(bf16[1024,768]{1,0:T(8,128)(2,1)} %get-tuple-element.438), channel_id=1, source_target_pairs={{0,2},{2,4},{4,6},{6,8},{8,10},{10,12},{12,14},{14,16},{16,18},{18... | collective-permute-start | bytes 4718600 | tf_op jit(solution)/shard_map/while/body/eval_jaxpr/ppermute | solution.py:17
  55.4 22.8 %collective-permute-start.1 = (bf16[1024,768]{1,0:T(8,128)(2,1)}, bf16[1024,768]{1,0:T(8,128)(2,1)}, u32[]{:S(2)}, u32[]{:S(2)}) collective-permute-start(bf16[1024,768]{1,0:T(8,128)(2,1)} %get-tuple-element.439), channel_id=1, source_target_pairs={{2,0},{4,2},{6,4},{8,6},{10,8},{12,10},{14,12},{16,14},{18,16},{20... | collective-permute-start | bytes 4718600 | tf_op jit(solution)/shard_map/while/body/eval_jaxpr/ppermute | solution.py:17
  84.8 36.9 %collective-permute-start = (bf16[1024,768]{1,0:T(8,128)(2,1)}, bf16[1024,768]{1,0:T(8,128)(2,1)S(1)}, u32[]{:S(2)}, u32[]{:S(2)}) collective-permute-start(bf16[1024,768]{1,0:T(8,128)(2,1)} %get-tuple-element.438), channel_id=1, source_target_pairs={{0,2},{2,4},{4,6},{6,8},{8,10},{10,12},{12,14},{14,16},{16,18},{18... | collective-permute-start | bytes 4718600 | tf_op jit(solution)/shard_map/while/body/eval_jaxpr/ppermute | solution.py:17
  118.4 20.2 %collective-permute-start.1 = (bf16[1024,768]{1,0:T(8,128)(2,1)}, bf16[1024,768]{1,0:T(8,128)(2,1)}, u32[]{:S(2)}, u32[]{:S(2)}) collective-permute-start(bf16[1024,768]{1,0:T(8,128)(2,1)} %get-tuple-element.439), channel_id=1, source_target_pairs={{2,0},{4,2},{6,4},{8,6},{10,8},{12,10},{14,12},{16,14},{18,16},{20... | collective-permute-start | bytes 4718600 | tf_op jit(solution)/shard_map/while/body/eval_jaxpr/ppermute | solution.py:17
  145.3 23.2 %collective-permute-start = (bf16[1024,768]{1,0:T(8,128)(2,1)}, bf16[1024,768]{1,0:T(8,128)(2,1)S(1)}, u32[]{:S(2)}, u32[]{:S(2)}) collective-permute-start(bf16[1024,768]{1,0:T(8,128)(2,1)} %get-tuple-element.438), channel_id=1, source_target_pairs={{0,2},{2,4},{4,6},{6,8},{8,10},{10,12},{12,14},{14,16},{16,18},{18... | collective-permute-start | bytes 4718600 | tf_op jit(solution)/shard_map/while/body/eval_jaxpr/ppermute | solution.py:17
  149.1 21.2 %collective-permute-start.1 = (bf16[1024,768]{1,0:T(8,128)(2,1)}, bf16[1024,768]{1,0:T(8,128)(2,1)}, u32[]{:S(2)}, u32[]{:S(2)}) collective-permute-start(bf16[1024,768]{1,0:T(8,128)(2,1)} %get-tuple-element.439), channel_id=1, source_target_pairs={{2,0},{4,2},{6,4},{8,6},{10,8},{12,10},{14,12},{16,14},{18,16},{20... | collective-permute-start | bytes 4718600 | tf_op jit(solution)/shard_map/while/body/eval_jaxpr/ppermute | solution.py:17
  176.9 36.9 %collective-permute-start = (bf16[1024,768]{1,0:T(8,128)(2,1)}, bf16[1024,768]{1,0:T(8,128)(2,1)S(1)}, u32[]{:S(2)}, u32[]{:S(2)}) collective-permute-start(bf16[1024,768]{1,0:T(8,128)(2,1)} %get-tuple-element.438), channel_id=1, source_target_pairs={{0,2},{2,4},{4,6},{6,8},{8,10},{10,12},{12,14},{14,16},{16,18},{18... | collective-permute-start | bytes 4718600 | tf_op jit(solution)/shard_map/while/body/eval_jaxpr/ppermute | solution.py:17
  210.5 20.2 %collective-permute-start.1 = (bf16[1024,768]{1,0:T(8,128)(2,1)}, bf16[1024,768]{1,0:T(8,128)(2,1)}, u32[]{:S(2)}, u32[]{:S(2)}) collective-permute-start(bf16[1024,768]{1,0:T(8,128)(2,1)} %get-tuple-element.439), channel_id=1, source_target_pairs={{2,0},{4,2},{6,4},{8,6},{10,8},{12,10},{14,12},{16,14},{18,16},{20... | collective-permute-start | bytes 4718600 | tf_op jit(solution)/shard_map/while/body/eval_jaxpr/ppermute | solution.py:17
  448.7 637.8 %reduce-scatter.13.cloned.1.call-start = ((), (), s32[]{:S(2)}) async-start(), calls=%async_computation.14 | async-start | bytes 2506752 | tf_op jit(solution)/shard_map/reduce_scatter | solution.py:290
  528.0 149.2 %all-to-all-start.5 = ((bf16[2,512,384]{1,2,0:T(8,128)(2,1)}), bf16[2,512,384]{1,2,0:T(8,128)(2,1)S(1)}, u32[]{:S(2)}, u32[]{:S(2)}) async-start(bf16[2,512,384]{1,2,0:T(8,128)(2,1)} %copy.185), calls=%async_computation.5 | async-start | bytes 1572864 | tf_op jit(solution)/shard_map/all_to_all | solution.py:264
  531.6 556.5 %reduce-scatter.19.cloned.1.call-start = ((), (), s32[]{:S(2)}) async-start(), calls=%async_computation.17 | async-start | bytes 2506752
  682.1 407.7 %reduce-scatter.21.cloned.1.call-start = ((), (), s32[]{:S(2)}) async-start(), calls=%async_computation.18 | async-start | bytes 2506752
  787.5 24.7 %collective-permute-start.3 = (bf16[1024,768]{1,0:T(8,128)(2,1)S(1)}, bf16[1024,768]{1,0:T(8,128)(2,1)}, u32[]{:S(2)}, u32[]{:S(2)}) collective-permute-start(bf16[1024,768]{1,0:T(8,128)(2,1)S(1)} %get-tuple-element.426), channel_id=1, source_target_pairs={{0,2},{2,4},{4,6},{6,8},{8,10},{10,12},{12,14},{14,16},{16,18},{18... | collective-permute-start | bytes 4718600 | tf_op jit(solution)/shard_map/while/body/eval_jaxpr/ppermute | solution.py:17
  822.2 21.6 %collective-permute-start.2 = (bf16[1024,768]{1,0:T(8,128)(2,1)}, bf16[1024,768]{1,0:T(8,128)(2,1)}, u32[]{:S(2)}, u32[]{:S(2)}) collective-permute-start(bf16[1024,768]{1,0:T(8,128)(2,1)} %get-tuple-element.425), channel_id=1, source_target_pairs={{2,0},{4,2},{6,4},{8,6},{10,8},{12,10},{14,12},{16,14},{18,16},{20... | collective-permute-start | bytes 4718600 | tf_op jit(solution)/shard_map/while/body/eval_jaxpr/ppermute | solution.py:17
  824.1 38.4 %collective-permute-start.3 = (bf16[1024,768]{1,0:T(8,128)(2,1)S(1)}, bf16[1024,768]{1,0:T(8,128)(2,1)}, u32[]{:S(2)}, u32[]{:S(2)}) collective-permute-start(bf16[1024,768]{1,0:T(8,128)(2,1)S(1)} %get-tuple-element.426), channel_id=1, source_target_pairs={{0,2},{2,4},{4,6},{6,8},{8,10},{10,12},{12,14},{14,16},{16,18},{18... | collective-permute-start | bytes 4718600 | tf_op jit(solution)/shard_map/while/body/eval_jaxpr/ppermute | solution.py:17
  872.5 23.5 %collective-permute-start.2 = (bf16[1024,768]{1,0:T(8,128)(2,1)}, bf16[1024,768]{1,0:T(8,128)(2,1)}, u32[]{:S(2)}, u32[]{:S(2)}) collective-permute-start(bf16[1024,768]{1,0:T(8,128)(2,1)} %get-tuple-element.425), channel_id=1, source_target_pairs={{2,0},{4,2},{6,4},{8,6},{10,8},{12,10},{14,12},{16,14},{18,16},{20... | collective-permute-start | bytes 4718600 | tf_op jit(solution)/shard_map/while/body/eval_jaxpr/ppermute | solution.py:17
  874.4 36.4 %collective-permute-start.3 = (bf16[1024,768]{1,0:T(8,128)(2,1)S(1)}, bf16[1024,768]{1,0:T(8,128)(2,1)}, u32[]{:S(2)}, u32[]{:S(2)}) collective-permute-start(bf16[1024,768]{1,0:T(8,128)(2,1)S(1)} %get-tuple-element.426), channel_id=1, source_target_pairs={{0,2},{2,4},{4,6},{6,8},{8,10},{10,12},{12,14},{14,16},{16,18},{18... | collective-permute-start | bytes 4718600 | tf_op jit(solution)/shard_map/while/body/eval_jaxpr/ppermute | solution.py:17
  920.8 25.0 %collective-permute-start.2 = (bf16[1024,768]{1,0:T(8,128)(2,1)}, bf16[1024,768]{1,0:T(8,128)(2,1)}, u32[]{:S(2)}, u32[]{:S(2)}) collective-permute-start(bf16[1024,768]{1,0:T(8,128)(2,1)} %get-tuple-element.425), channel_id=1, source_target_pairs={{2,0},{4,2},{6,4},{8,6},{10,8},{12,10},{14,12},{16,14},{18,16},{20... | collective-permute-start | bytes 4718600 | tf_op jit(solution)/shard_map/while/body/eval_jaxpr/ppermute | solution.py:17
  922.7 26.4 %collective-permute-start.3 = (bf16[1024,768]{1,0:T(8,128)(2,1)S(1)}, bf16[1024,768]{1,0:T(8,128)(2,1)}, u32[]{:S(2)}, u32[]{:S(2)}) collective-permute-start(bf16[1024,768]{1,0:T(8,128)(2,1)S(1)} %get-tuple-element.426), channel_id=1, source_target_pairs={{0,2},{2,4},{4,6},{6,8},{8,10},{10,12},{12,14},{14,16},{16,18},{18... | collective-permute-start | bytes 4718600 | tf_op jit(solution)/shard_map/while/body/eval_jaxpr/ppermute | solution.py:17
  973.5 147.6 %reduce-scatter.23.cloned.1.call-start = ((), (), s32[]{:S(2)}) async-start(), calls=%async_computation.19 | async-start | bytes 2506752
  993.1 242.3 %reduce-scatter.17.cloned.1.call-start = ((), (), s32[]{:S(2)}) async-start(), calls=%async_computation.16 | async-start | bytes 10027008 | tf_op jit(solution)/shard_map/reduce_scatter | solution.py:294
  1004.1 346.9 %reduce-scatter.15.cloned.1.call-start = ((), (), s32[]{:S(2)}) async-start(), calls=%async_computation.15 | async-start | bytes 10027008 | tf_op jit(solution)/shard_map/reduce_scatter | solution.py:293
  1012.9 388.3 %all-reduce.10.cloned.1.call-start = ((), (), s32[]{:S(2)}) async-start(), calls=%async_computation.20 | async-start | bytes 2506752 | tf_op jit(solution)/shard_map/psum | solution.py:299
  (81 other events, 1838.5 us)
Sparse Core Ops, SparseCore 0:
  462.9 65.5 reduce-scatter.12
  682.2 65.9 reduce-scatter.18
  973.6 81.4 reduce-scatter.20
  1059.1 61.8 reduce-scatter.22
  1125.0 110.3 reduce-scatter.16
  1239.9 111.1 reduce-scatter.14
  1354.9 46.3 all-reduce.9
where the time goes:
time: 1430 us; the launch traced here: 1420 us
  waiting for transfers between devices  434 us (30%)
  local copies, waits for them, and re-layouts  339 us (24%)
  other arithmetic  193 us (13%)
  starting transfers between devices  178 us (12%)
  matrix products  164 us (11%)
  blocking collectives  94.6 us (7%)
  between operations  16.2 us (1%)
    ppermute x16, starting transfers between devices, shifted(): lax.ppermute(value, axis, [(source, source + steps) for source in range(f...  155 us
    ppermute x16, waiting for transfers between devices, shifted(): lax.ppermute(value, axis, [(source, source + steps) for source in range(f...  118 us
    reduce_scatter x1, waiting for transfers between devices, body(): lax.psum_scatter(grad_terms[6], 'seq', scatter_dimension=0, tiled=True)  114 us
    reduce_scatter x1, waiting for transfers between devices, body(): lax.psum_scatter(grad_terms[7], 'seq', scatter_dimension=0, tiled=True)  113 us
    unnamed x1, blocking collectives  64.5 us
    scatter-add x1, other arithmetic, body(): grad_buffer.at[local_rows.reshape(-1)]  63.8 us
    unnamed x169, local copies, waits for them, and re-layouts  56 us
    concatenate x2, local copies, waits for them, and re-layouts, body(): jnp.concatenate([grad_key_rows.reshape(stretch_blocks, slot_count, BLK, -...  50.3 us
  transfers between devices with their start and end apart: 29, of which 22 were waited for; matrix products, arithmetic and copies ran while one was open for 40% of the time, Pallas kernels for 0%

commit v1 on v0

v1 whole, which is shorter than its diff:
```python
import functools

import jax
import jax.numpy as jnp
from jax import lax
from jax.experimental import pallas as pl
from jax.experimental.pallas import tpu as pltpu
from jax.sharding import PartitionSpec as P

DH = 64
BLK = 64
MAXB = 64
SLOTS = 8
HG = 3
WQ = HG * DH
WIN = 256
AXES = ("seq", "head")
NEG = -1e30

eps_norm = 1e-06


def xor_swap(value, bits):
    count = lax.axis_size("seq") * lax.axis_size("head")
    return lax.ppermute(value, AXES, [(d, d ^ bits) for d in range(count)])


def plane_shift(value, steps):
    count = lax.axis_size("seq") * lax.axis_size("head")
    gap = 8 * steps
    return lax.ppermute(
        value, AXES, [(d, d + gap) for d in range(count) if 0 <= d + gap < count]
    )


def block_slots(blocks, rand_rows, lengths, seq_order):
    seq_count = lengths.shape[0]
    seq_ids = jnp.arange(seq_count, dtype=jnp.int32)
    packed = jnp.sum(jnp.where(seq_order[:, None] == seq_ids[None, :], lengths[None, :], 0), axis=1)
    seq_ends = jnp.cumsum(packed)
    starts = seq_ends - packed
    holder = jnp.sum((seq_ends[None, :] <= blocks[:, None]).astype(jnp.int32), axis=1)
    chosen = holder[:, None] == seq_ids[None, :]
    seq_first = jnp.sum(jnp.where(chosen, starts[None, :], 0), axis=1)
    seq_span = jnp.sum(jnp.where(chosen, packed[None, :], 0), axis=1)
    offset = blocks - seq_first
    rand_pos = seq_first[:, None] + jnp.mod(rand_rows, seq_span[:, None])
    fixed_cand = jnp.stack(
        [blocks - 1, blocks, blocks + 1, seq_first, seq_first + seq_span - 1], axis=1
    )
    candidate = jnp.concatenate([fixed_cand, rand_pos], axis=1)
    fixed_live = jnp.stack(
        [offset > 0, offset >= 0, offset < seq_span - 1, offset >= 0, offset >= 0], axis=1
    )
    usable = jnp.concatenate([fixed_live, rand_pos >= 0], axis=1)
    kept_list = []
    for column in range(candidate.shape[1]):
        unique = usable[:, column]
        for earlier in range(column):
            unique = unique & jnp.logical_not(
                kept_list[earlier] & (candidate[:, earlier] == candidate[:, column])
            )
        kept_list.append(unique)
    is_live = jnp.stack(kept_list, axis=1)
    key_blocks = jnp.where(is_live, candidate, blocks[:, None])
    return (key_blocks, is_live)


def norm_forward(values, gain_vec, shift_vec):
    center = values - jnp.mean(values, axis=-1, keepdims=True)
    spread = jnp.mean(center * center, axis=-1, keepdims=True)
    inv_dev = lax.rsqrt(spread + eps_norm)
    x_hat = center * inv_dev
    return (x_hat * gain_vec + shift_vec, x_hat, inv_dev)


def norm_backward(grad_in, x_hat, inv_dev, gain_vec):
    grad_gain = jnp.sum(grad_in * x_hat, axis=0)
    grad_shift = jnp.sum(grad_in, axis=0)
    grad_hat = grad_in * gain_vec
    grad_mean = jnp.mean(grad_hat, axis=-1, keepdims=True)
    grad_proj = jnp.mean(grad_hat * x_hat, axis=-1, keepdims=True)
    return (inv_dev * (grad_hat - grad_mean - x_hat * grad_proj), grad_gain, grad_shift)


def gelu_tanh(values):
    return jax.nn.gelu(values, approximate=True)


def lane_groups(rows, offset):
    lane = lax.broadcasted_iota(jnp.int32, (rows, WIN), 1) - offset
    return [jnp.logical_and(lane >= h * DH, lane < (h + 1) * DH) for h in range(HG)]


def spread_heads(block, offset):
    zero = jnp.zeros_like(block)
    return jnp.concatenate([jnp.where(m, block, zero) for m in lane_groups(BLK, offset)], axis=0)


def fold_heads(stacked, offset):
    masks = lane_groups(BLK, offset)
    total = jnp.where(masks[0], stacked[:BLK], 0.0)
    for h in range(1, HG):
        total = total + jnp.where(masks[h], stacked[h * BLK : (h + 1) * BLK], 0.0)
    return total


def fetch(pieces, kv, sems):
    rows = pieces[0].shape[0]
    for n, piece in enumerate(pieces):
        pltpu.make_async_copy(piece, kv.at[pl.ds(n * rows, rows)], sems.at[n]).start()
    for n, piece in enumerate(pieces):
        pltpu.make_async_copy(piece, kv.at[pl.ds(n * rows, rows)], sems.at[n]).wait()


def nt(a, b):
    return lax.dot_general(a, b, (((1,), (1,)), ((), ())), preferred_element_type=jnp.float32)


def tn(a, b):
    return lax.dot_general(a, b, (((0,), (0,)), ((), ())), preferred_element_type=jnp.float32)


def forward_kernel(idx_ref, bias_ref, q_ref, *refs):
    pieces, ctx_ref, kv, sems = refs[:6], refs[6], refs[7], refs[8]
    fetch(pieces, kv, sems)

    def step(i, carry):
        q_rows = pl.multiple_of(i * BLK, BLK)
        qexp = spread_heads(q_ref[pl.ds(q_rows, BLK), :], 0)
        rows = [
            pl.multiple_of(idx_ref[i * SLOTS + s] * BLK, BLK) for s in range(SLOTS)
        ]
        keys = jnp.concatenate([kv[pl.ds(r, BLK), 0:WIN] for r in rows], axis=0)
        values = jnp.concatenate([kv[pl.ds(r, BLK), 128 : 128 + WIN] for r in rows], axis=0)
        scores = nt(qexp, keys) + bias_ref[pl.ds(i, 1), :]
        top = jnp.max(scores, axis=1, keepdims=True)
        e = jnp.exp(scores - top)
        total = jnp.sum(e, axis=1, keepdims=True)
        out = jnp.dot(e.astype(jnp.bfloat16), values, preferred_element_type=jnp.float32)
        ctx_ref[pl.ds(q_rows, BLK), :] = fold_heads(out / total, 64).astype(jnp.bfloat16)
        return carry

    lax.fori_loop(0, q_ref.shape[0] // BLK, step, 0)


def backward_kernel(idx_ref, live_ref, q_ref, do_ref, *refs):
    pieces, dq_ref, outs = refs[:6], refs[6], refs[7:13]
    kv, acc, sems = refs[13:]
    rows_piece = pieces[0].shape[0]

    def clear(n, carry):
        acc[pl.ds(pl.multiple_of(n * 256, 256), 256), :] = jnp.zeros((256, 2 * WQ), jnp.float32)
        return carry

    for n, piece in enumerate(pieces):
        pltpu.make_async_copy(piece, kv.at[pl.ds(n * rows_piece, rows_piece)], sems.at[n]).start()
    lax.fori_loop(0, acc.shape[0] // 256, clear, 0)
    for n, piece in enumerate(pieces):
        pltpu.make_async_copy(piece, kv.at[pl.ds(n * rows_piece, rows_piece)], sems.at[n]).wait()

    def step(i, carry):
        q_rows = pl.multiple_of(i * BLK, BLK)
        qexp = spread_heads(q_ref[pl.ds(q_rows, BLK), :], 0)
        doexp = spread_heads(do_ref[pl.ds(q_rows, BLK), :], 64)
        rows = [
            pl.multiple_of(idx_ref[i * SLOTS + s] * BLK, BLK) for s in range(SLOTS)
        ]
        keys = jnp.concatenate([kv[pl.ds(r, BLK), 0:WIN] for r in rows], axis=0)
        values = jnp.concatenate([kv[pl.ds(r, BLK), 128 : 128 + WIN] for r in rows], axis=0)
        raw = nt(keys, qexp)
        scores = jnp.concatenate(
            [
                jnp.where(live_ref[i * SLOTS + s] > 0, raw[s * BLK : (s + 1) * BLK], NEG)
                for s in range(SLOTS)
            ],
            axis=0,
        )
        top = jnp.max(scores, axis=0, keepdims=True)
        e = jnp.exp(scores - top)
        probs = e * (1.0 / jnp.sum(e, axis=0, keepdims=True))
        grad_probs = nt(values, doexp)
        inner = jnp.sum(probs * grad_probs, axis=0, keepdims=True)
        grad_scores = (probs * (grad_probs - inner)).astype(jnp.bfloat16)
        dk = jnp.dot(grad_scores, qexp, preferred_element_type=jnp.float32)
        dv = jnp.dot(probs.astype(jnp.bfloat16), doexp, preferred_element_type=jnp.float32)
        dq = tn(grad_scores, keys)
        dq_ref[pl.ds(q_rows, BLK), :] = (fold_heads(dq, 0) * DH ** (-0.5)).astype(jnp.bfloat16)
        for s in range(SLOTS):
            k_s, v_s = dk[s * BLK : (s + 1) * BLK], dv[s * BLK : (s + 1) * BLK]
            at = pl.ds(rows[s], BLK)
            acc[at, 0:128] += k_s[:, :128]
            acc[at, 128:256] += k_s[:, 128:] + v_s[:, :128]
            acc[at, 256:384] += v_s[:, 128:]
        return carry

    lax.fori_loop(0, q_ref.shape[0] // BLK, step, 0)

    def emit(n, carry):
        at = pl.multiple_of(n * 256, 256)
        for j in range(6):
            part = acc[pl.ds(j * rows_piece + at, 256), :]
            outs[j][pl.ds(at, 256), :] = part.astype(jnp.bfloat16)
        return carry

    lax.fori_loop(0, rows_piece // 256, emit, 0)


VMEM = pl.BlockSpec(memory_space=pltpu.VMEM)
SMEM = pl.BlockSpec(memory_space=pltpu.SMEM)
ANY = pl.BlockSpec(memory_space=pl.ANY)


def attend(idx, bias, queries, pieces):
    rows, width = pieces[0].shape
    count = queries.shape[0]
    return pl.pallas_call(
        forward_kernel,
        out_shape=jax.ShapeDtypeStruct((count, WIN), jnp.bfloat16),
        in_specs=[SMEM, VMEM, VMEM] + [ANY] * 6,
        out_specs=VMEM,
        scratch_shapes=[
            pltpu.VMEM((6 * rows, width), jnp.bfloat16),
            pltpu.SemaphoreType.DMA((6,)),
        ],
        compiler_params=pltpu.CompilerParams(vmem_limit_bytes=24 << 20),
        cost_estimate=pl.CostEstimate(
            flops=2 * 4 * count * 3 * 256 * 512, bytes_accessed=12 * rows * width, transcendentals=count * 3 * 512
        ),
        name="attend",
    )(idx, bias, queries, *pieces)


def attend_back(idx, live, queries, grads, pieces):
    rows, width = pieces[0].shape
    count = queries.shape[0]
    kv_shape = jax.ShapeDtypeStruct((rows, width), jnp.bfloat16)
    return pl.pallas_call(
        backward_kernel,
        out_shape=[jax.ShapeDtypeStruct((count, WIN), jnp.bfloat16)] + [kv_shape] * 6,
        in_specs=[SMEM, SMEM, VMEM, VMEM] + [ANY] * 6,
        out_specs=[VMEM] * 7,
        scratch_shapes=[
            pltpu.VMEM((6 * rows, width), jnp.bfloat16),
            pltpu.VMEM((6 * rows, width), jnp.float32),
            pltpu.SemaphoreType.DMA((6,)),
        ],
        compiler_params=pltpu.CompilerParams(vmem_limit_bytes=56 << 20),
        cost_estimate=pl.CostEstimate(
            flops=2 * 10 * count * 3 * 256 * 512, bytes_accessed=24 * rows * width, transcendentals=count * 3 * 512
        ),
        name="attend_back",
    )(idx, live, queries, grads, *pieces)


def add_low(*terms):
    total = terms[0].astype(jnp.float32)
    for term in terms[1:]:
        total = total + term.astype(jnp.float32)
    return total


def pick(array, at, axis):
    return lax.dynamic_index_in_dim(array, at, axis, keepdims=False)


def plane_sum(slabs, plane, count):
    terms = [pick(slabs, plane, 0)]
    for gap in range(1, count):
        up = pick(slabs, jnp.minimum(plane + gap, count - 1), 0)
        down = pick(slabs, jnp.maximum(plane - gap, 0), 0)
        terms.append(plane_shift(up, gap))
        terms.append(plane_shift(down, -gap))
    return add_low(*terms)


def core_half(slabs, core, axis):
    got = xor_swap(pick(slabs, 1 - core, axis), 2)
    return add_low(pick(slabs, core, axis), got).astype(jnp.bfloat16)


def body(
    tokens,
    w_query,
    w_key,
    w_value,
    w_out,
    gain_attn,
    shift_attn,
    w_up,
    w_down,
    gain_mlp,
    shift_mlp,
    cotangent,
    lengths,
    seq_order,
    rand_blocks,
):
    piece, width = tokens.shape
    seqs, heads = lax.axis_size("seq"), lax.axis_size("head")
    planes = seqs // 4
    piece_blocks = piece // BLK
    assert heads == 2 and 8 * piece == MAXB * BLK and width == 4 * WQ
    seq_at, x_at = lax.axis_index("seq"), lax.axis_index("head")
    plane, y_at, core = seq_at // 4, (seq_at // 2) % 2, seq_at % 2
    group = y_at * 2 + x_at

    from_x = xor_swap(tokens, 1)
    from_y = xor_swap(tokens, 4)
    from_xy = xor_swap(tokens, 5)
    rand_y = lax.ppermute(rand_blocks, "seq", [(s, s ^ 2) for s in range(seqs)])

    def columns(weights):
        return lax.dynamic_slice_in_dim(weights, group * WQ, WQ, 1)

    wq_own = jnp.pad(columns(w_query) * jnp.bfloat16(DH ** (-0.5)), ((0, 0), (0, WIN - WQ)))
    wkv_own = jnp.concatenate([columns(w_key), columns(w_value)], axis=1)
    order = [group ^ j for j in range(4)]
    wout_own = jnp.concatenate(
        [
            jnp.pad(lax.dynamic_slice_in_dim(w_out, g * WQ, WQ, 0), ((WIN - WQ, 0), (0, 0)))
            for g in order
        ],
        axis=0,
    )

    local = jnp.arange(4 * piece_blocks, dtype=jnp.int32)
    far, near = local // piece_blocks, local % piece_blocks
    half = 4 * piece_blocks
    blocks = (
        plane * MAXB
        + (y_at ^ (far >> 1)) * half
        + core * (2 * piece_blocks)
        + (x_at ^ (far & 1)) * piece_blocks
        + near
    )
    here = rand_blocks.reshape(2, piece_blocks, -1)
    there = rand_y.reshape(2, piece_blocks, -1)
    rand_rows = jnp.concatenate(
        [pick(here, x_at, 0), pick(here, 1 - x_at, 0), pick(there, x_at, 0), pick(there, 1 - x_at, 0)],
        axis=0,
    )
    key_blocks, is_live = block_slots(blocks, rand_rows, lengths, seq_order)
    rel = key_blocks // MAXB - plane + 1
    in_plane = key_blocks % MAXB
    y_of, rest = in_plane // half, in_plane % half
    core_of, rest = rest // (2 * piece_blocks), rest % (2 * piece_blocks)
    x_of, near_of = rest // piece_blocks, rest % piece_blocks
    idx = (
        ((rel * 2 + (core_of ^ core)) * 4 + ((y_of ^ y_at) * 2 + (x_of ^ x_at))) * piece_blocks
        + near_of
    ).reshape(-1)
    live = is_live.astype(jnp.int32).reshape(-1)
    bias = jnp.repeat(jnp.where(is_live, 0.0, NEG).astype(jnp.float32), BLK, axis=1)

    def low_dot(a, b):
        return jnp.dot(a, b, preferred_element_type=jnp.float32).astype(jnp.bfloat16)

    stretch = jnp.concatenate([tokens, from_x, from_y, from_xy], axis=0)
    kv_own = low_dot(stretch, wkv_own)
    queries = low_dot(stretch, wq_own)
    kv_below = plane_shift(kv_own, 1)
    kv_above = plane_shift(kv_own, -1)
    pieces = [
        kv_below,
        xor_swap(kv_below, 2),
        kv_own,
        xor_swap(kv_own, 2),
        kv_above,
        xor_swap(kv_above, 2),
    ]
    context = attend(idx, bias, queries, pieces)

    def to_owners(array):
        parts = array.reshape(4, piece, -1)
        return [parts[0], xor_swap(parts[1], 1), xor_swap(parts[2], 4), xor_swap(parts[3], 5)]

    context_tok = jnp.concatenate(to_owners(context), axis=1)
    attn_out = jnp.dot(context_tok, wout_own, preferred_element_type=jnp.float32)
    normed, hat_one, dev_one = norm_forward(
        tokens.astype(jnp.float32) + attn_out, gain_attn, shift_attn
    )
    normed_low = normed.astype(jnp.bfloat16)
    hidden_pre = jnp.dot(normed_low, w_up, preferred_element_type=jnp.float32)
    hidden = gelu_tanh(hidden_pre).astype(jnp.bfloat16)
    mlp_out = jnp.dot(hidden, w_down, preferred_element_type=jnp.float32)
    output, hat_two, dev_two = norm_forward(normed + mlp_out, gain_mlp, shift_mlp)
    grad_two, grad_gain_mlp, grad_shift_mlp = norm_backward(
        cotangent.astype(jnp.float32), hat_two, dev_two, gain_mlp
    )
    grad_mlp = grad_two.astype(jnp.bfloat16)
    grad_hidden = jnp.dot(grad_mlp, w_down.T, preferred_element_type=jnp.float32)
    gelu_out, gelu_pull = jax.vjp(gelu_tanh, hidden_pre)
    grad_pre = gelu_pull(grad_hidden)[0].astype(jnp.bfloat16)
    grad_normed = grad_two + jnp.dot(grad_pre, w_up.T, preferred_element_type=jnp.float32)
    grad_one, grad_gain_attn, grad_shift_attn = norm_backward(
        grad_normed, hat_one, dev_one, gain_attn
    )
    grad_attn = grad_one.astype(jnp.bfloat16)
    grad_context = low_dot(grad_attn, wout_own.T)
    cols = [grad_context[:, j * WIN : (j + 1) * WIN] for j in range(4)]
    grad_ctx = jnp.concatenate(
        [cols[0], xor_swap(cols[1], 1), xor_swap(cols[2], 4), xor_swap(cols[3], 5)], axis=0
    )

    grad_w_down = low_dot(hidden.T, grad_mlp)
    grad_w_up = low_dot(normed_low.T, grad_pre)
    grad_w_out = low_dot(context_tok.T, grad_attn).reshape(4, WIN, width)[:, WIN - WQ :]
    grad_w_out = jnp.concatenate([pick(grad_w_out, g, 0) for g in order], axis=0)

    norm_rows = jnp.stack([grad_gain_attn, grad_shift_attn, grad_gain_mlp, grad_shift_mlp])
    share = width // seqs
    norm_rows = norm_rows.reshape(4, seqs, share).transpose(1, 0, 2).reshape(seqs, 1, 4 * share)
    norm_rows = jnp.pad(norm_rows, ((0, 0), (0, 15), (0, width - 4 * share))).astype(jnp.bfloat16)
    out_slabs = jnp.concatenate([grad_w_out.reshape(seqs, share, width), norm_rows], axis=1)
    up_slabs = grad_w_up.reshape(seqs, share, -1)
    down_slabs = grad_w_down.reshape(seqs, -1, width)

    def y_then_x(slabs):
        slabs = slabs.reshape((planes, 2, 2) + slabs.shape[1:])
        slabs = core_half(slabs, core, 2)
        got = xor_swap(pick(slabs, 1 - y_at, 1), 4)
        slabs = add_low(pick(slabs, y_at, 1), got).astype(jnp.bfloat16)
        mine = plane_sum(slabs, plane, planes).astype(jnp.bfloat16)
        return add_low(mine, xor_swap(mine, 1))

    def x_then_y(slabs):
        slabs = slabs.reshape((planes, 2, 2) + slabs.shape[1:])
        slabs = core_half(slabs, core, 2)
        slabs = slabs.reshape(planes, 2, 2, slabs.shape[2] // 2, -1)
        got = xor_swap(pick(slabs, 1 - x_at, 2), 1)
        slabs = add_low(pick(slabs, x_at, 2), got).astype(jnp.bfloat16)
        got = xor_swap(pick(slabs, 1 - y_at, 1), 4)
        slabs = add_low(pick(slabs, y_at, 1), got).astype(jnp.bfloat16)
        mine = plane_sum(slabs, plane, planes).astype(jnp.bfloat16)
        other = xor_swap(mine, 1)
        low_x = x_at == 0
        return jnp.concatenate(
            [jnp.where(low_x, mine, other), jnp.where(low_x, other, mine)], axis=0
        ).astype(jnp.float32)

    down_total = x_then_y(down_slabs)
    up_total = y_then_x(up_slabs)
    out_total = y_then_x(out_slabs)

    back = attend_back(idx, live, queries, grad_ctx, pieces)
    grad_q, kv_parts = back[0], back[1:]
    sums = [add_low(kv_parts[2 * r], xor_swap(kv_parts[2 * r + 1], 2)) for r in range(3)]
    grad_kv = (
        sums[1]
        + plane_shift(sums[0].astype(jnp.bfloat16), -1).astype(jnp.float32)
        + plane_shift(sums[2].astype(jnp.bfloat16), 1).astype(jnp.float32)
    ).astype(jnp.bfloat16)
    wq_plain = jnp.pad(columns(w_query), ((0, 0), (0, WIN - WQ)))
    grad_stretch = jnp.dot(grad_q, wq_plain.T, preferred_element_type=jnp.float32) + jnp.dot(
        grad_kv, wkv_own.T, preferred_element_type=jnp.float32
    )
    sent = grad_stretch.astype(jnp.bfloat16).reshape(4, piece, width)
    grad_tokens = grad_one + grad_stretch[:piece] + add_low(
        xor_swap(sent[1], 1), xor_swap(sent[2], 4), xor_swap(sent[3], 5)
    )

    grad_wq = low_dot(stretch.T, grad_q)[:, :WQ]
    grad_wkv = low_dot(stretch.T, grad_kv)
    proj = jnp.concatenate([grad_wq, grad_wkv], axis=1).reshape(planes, 2, 2, share, 3 * WQ)
    proj = core_half(proj, core, 2)
    proj = plane_sum(proj, plane, planes).astype(jnp.bfloat16)
    kept, given = pick(proj, y_at, 0), pick(proj, 1 - y_at, 0)
    quarters = jnp.stack([kept, xor_swap(kept, 1), xor_swap(given, 4), xor_swap(given, 5)])
    quarters = [pick(quarters, g, 0) for g in order]

    def whole(n):
        return jnp.concatenate([q[:, n * WQ : (n + 1) * WQ] for q in quarters], axis=1).astype(
            jnp.float32
        )

    norm_row = out_total[share]

    def norm_grad(n):
        return norm_row[n * share : (n + 1) * share]

    return (
        output.astype(jnp.bfloat16),
        grad_tokens,
        whole(0),
        whole(1),
        whole(2),
        out_total[:share],
        norm_grad(0),
        norm_grad(1),
        up_total,
        down_total,
        norm_grad(2),
        norm_grad(3),
    )


def solution(mesh):
    rows = P(("seq", "head"), None)
    seq_rows, seq_only = P("seq", None), P("seq")
    return jax.shard_map(
        body,
        mesh=mesh,
        in_specs=(rows,) + (P(),) * 10 + (rows, P(), P(), seq_rows),
        out_specs=(
            rows,
            rows,
            seq_rows,
            seq_rows,
            seq_rows,
            seq_rows,
            seq_only,
            seq_only,
            seq_rows,
            seq_rows,
            seq_only,
            seq_only,
        ),
        check_vma=False,
    )
```

time: 1430 us -> 417 us (0.29)
  local copies, waits for them, and re-layouts: 339 us -> 19.5 us
  waiting for transfers between devices: 434 us -> 142 us
  other arithmetic: 193 us -> 23.4 us
  matrix products: 164 us -> 50.3 us
  blocking collectives: 94.6 us -> 0 us
  starting transfers between devices: 178 us -> 114 us
  Pallas kernels: 0 us -> 57.7 us
    reduce_scatter x3 -> x0, waiting for transfers between devices: 226 us -> none  [the longest x1 114 us: body(): lax.psum_scatter(grad_terms[6], 'seq', scatter_dimension=0, tiled=True)]
    convert_element_type x23 -> x20, other arithmetic: 85.6 us -> 10.7 us  [the longest x3 2.25 us: whole(): jnp.concatenate([q[:, n * WQ:(n + 1) * WQ] for q in quarters], axis=1)]
    dot_general x18 -> x11, matrix products: 105 us -> 31.3 us  [the longest x8 24.1 us: low_dot(): jnp.dot(a, b, preferred_element_type=jnp.float32).astype(jnp.bfloat16)]
    unnamed x1 -> x0, blocking collectives: 64.5 us -> none
    scatter-add x1 -> x0, other arithmetic: 63.8 us -> none  [body(): grad_buffer.at[local_rows.reshape(-1)]]
    pallas_call x0 -> x2, Pallas kernels: none -> 57.7 us  [the longest x1 38.7 us: attend_back(): pl.pallas_call(backward_kernel, out_shape=[jax.ShapeDtypeStruct((count, W...]
    unnamed x169 -> x87, local copies, waits for them, and re-layouts: 56 us -> 4.05 us
    concatenate x2, local copies, waits for them, and re-layouts: 50.3 us -> 1.58 us  [the longest x1 1.53 us: body(): jnp.concatenate([grad_wq, grad_wkv], axis=1)]
  transfers between devices with their start and end apart: 29 -> 61, of which waited for: 22 -> 21; matrix products, arithmetic and copies ran while one was open for 40% -> 12% of each run, Pallas kernels for 0% -> 9%
where the time goes in v1:
time: 417 us; the launch traced here: 409 us
  waiting for transfers between devices  142 us (34%)
  starting transfers between devices  114 us (27%)
  Pallas kernels  57.7 us (14%)
  matrix products  50.3 us (12%)
  other arithmetic  23.4 us (6%)
  local copies, waits for them, and re-layouts  19.5 us (5%)
    ppermute x28, starting transfers between devices, plane_shift(): lax.ppermute(value, AXES, [(d, d + gap) for d in range(count) if 0 <= d +...  87.4 us
    ppermute x32, waiting for transfers between devices, xor_swap(): return lax.ppermute(value, AXES, [(d, d ^ bits) for d in range(count)])  74.9 us
    ppermute x28, waiting for transfers between devices, plane_shift(): lax.ppermute(value, AXES, [(d, d + gap) for d in range(count) if 0 <= d +...  66.8 us
    pallas_call x1, Pallas kernels, attend_back(): pl.pallas_call(backward_kernel, out_shape=[jax.ShapeDtypeStruct((count, W...  38.7 us
    ppermute x32, starting transfers between devices, xor_swap(): return lax.ppermute(value, AXES, [(d, d ^ bits) for d in range(count)])  25.5 us
    dot_general x8, matrix products, low_dot(): jnp.dot(a, b, preferred_element_type=jnp.float32).astype(jnp.bfloat16)  24.1 us
    pallas_call x1, Pallas kernels, attend(): pl.pallas_call(forward_kernel, out_shape=jax.ShapeDtypeStruct((count, WIN...  19 us
  transfers between devices with their start and end apart: 61, of which 21 were waited for; matrix products, arithmetic and copies ran while one was open for 12% of the time, Pallas kernels for 9%

profile of v1, /device:TPU:24, one launch (start us, length us, event | category | flops | bytes accessed | tf_op | source)
XLA Modules:
  0.0 409.4 jit_solution(4925140574297599476)
XLA Ops:
  10.5 10.9 %collective-permute-done.1 = bf16[512,768]{1,0:T(8,128)(2,1)S(1)} collective-permute-done((bf16[512,768]{1,0:T(8,128)(2,1)}, bf16[512,768]{1,0:T(8,128)(2,1)S(1)}, u32[]{:S(2)}, u32[]{:S(2)}) %collective-permute-start.1) | collective-permute-done | bytes 786464 | tf_op jit(solution)/shard_map/ppermute | solution.py:25
  21.4 16.9 %collective-permute-done.2 = bf16[512,768]{1,0:T(8,128)(2,1)S(1)} collective-permute-done((bf16[512,768]{1,0:T(8,128)(2,1)}, bf16[512,768]{1,0:T(8,128)(2,1)S(1)}, u32[]{:S(2)}, u32[]{:S(2)}) %collective-permute-start.2) | collective-permute-done | bytes 786464 | tf_op jit(solution)/shard_map/ppermute | solution.py:25
  41.7 5.8 %collective-permute-start.7 = (bf16[2048,384]{1,0:T(8,128)(2,1)S(1)}, bf16[2048,384]{1,0:T(8,128)(2,1)}, u32[]{:S(2)}, u32[]{:S(2)}) collective-permute-start(bf16[2048,384]{1,0:T(8,128)(2,1)S(1)} %convolution_convert_fusion.2.refs_2_), channel_id=1, source_target_pairs={{8,0},{9,1},{10,2},{11,3},{12,4},{13,5},{14,6},{15,7},{16,8},{17,9... | collective-permute-start | bytes 4718600 | tf_op jit(solution)/shard_map/ppermute | solution.py:31
  50.0 27.2 %collective-permute-done.4.refs_0_ = bf16[2048,384]{1,0:T(8,128)(2,1)S(1)} collective-permute-done((bf16[2048,384]{1,0:T(8,128)(2,1)S(1)}, bf16[2048,384]{1,0:T(8,128)(2,1)S(1)}, u32[]{:S(2)}, u32[]{:S(2)}) %collective-permute-start.4) | collective-permute-done | bytes 1572896 | tf_op jit(solution)/shard_map/ppermute | solution.py:31
  83.2 19.0 %attend.1 = bf16[2048,256]{1,0:T(8,128)(2,1)S(1)} custom-call(s32[256]{0:T(256)S(1)} %fusion.72.idx_ref, f32[32,512]{1,0:T(8,128)S(1)} %reshape.488.bias_ref, bf16[2048,256]{1,0:T(8,128)(2,1)S(1)} %convolution_convert_fusion.3.q_ref, bf16[2048,384]{1,0:T(8,128)(2,1)S(1)} %collective-permute-done.4.refs_0_, bf16[2048,384]{1,0:T(8,128)(2,1)} %collective-permute-done.5.refs_1_, ...), custom_call_target="tpu_custom_call" | custom-call | flops 6442450944 | bytes 9437184 | tf_op jit(solution)/shard_map/attend/pallas_call | solution.py:217
  108.6 8.8 %collective-permute-done.10 = bf16[512,256]{1,0:T(8,128)(2,1)} collective-permute-done((bf16[512,256]{1,0:T(8,128)(2,1)}, bf16[512,256]{1,0:T(8,128)(2,1)}, u32[]{:S(2)}, u32[]{:S(2)}) %collective-permute-start.10) | collective-permute-done | bytes 262176 | tf_op jit(solution)/shard_map/ppermute | solution.py:25
  130.9 6.1 %convolution_convert_fusion = bf16[3072,768]{1,0:T(8,128)(2,1)} fusion(f32[512,3072]{1,0:T(8,128)S(1)} %fusion.83, bf16[512,768]{1,0:T(8,128)(2,1)S(1)} %copy-done.9, f32[512,768]{1,0:T(8,128)S(1)} %get-tuple-element.126, f32[512]{0:T(512)S(1)} %broadcast_multiply_fusion.3, f32[512]{0:T(512)S(1)} %broadcast_multiply_fusion.4, f32[768]{0:T(1024)S(1)} %copy-done.28, ...), kind=kOutput, calls=%fused_computation.10 | convolution fusion | flops 2435973120 | bytes 13380608 | tf_op jit(solution)/shard_map/dot_general | solution.py:357
  137.1 7.9 %fusion.6 = bf16[512,3072]{1,0:T(8,128)(2,1)S(1)} fusion(f32[512,3072]{1,0:T(8,128)S(1)} %fusion.83, bf16[3072,768]{1,0:T(8,128)(2,1)S(1)} %bitcast.254, bf16[512,768]{1,0:T(8,128)(2,1)S(1)} %copy-done.9, f32[512,768]{1,0:T(8,128)S(1)} %get-tuple-element.126, f32[512]{0:T(512)S(1)} %broadcast_multiply_fusion.3, f32[512]{0:T(512)S(1)} %broadcast_multiply_fusion.4, ...), kind=kOutput, calls=%fused_computation.8 | convolution fusion | flops 2450915328 | bytes 16526336 | tf_op jit(solution)/shard_map/dot_general | solution.py:392
  161.7 4.9 %convolution_convert_fusion.1 = bf16[768,3072]{1,0:T(8,128)(2,1)} fusion(bf16[512,3072]{1,0:T(8,128)(2,1)S(1)} %copy-done.34, f32[512,768]{1,0:T(8,128)S(1)} %get-tuple-element.124, f32[768]{0:T(1024)S(1)} %copy-done.32, f32[768]{0:T(1024)S(1)} %copy-done.29, f32[512]{0:T(512)S(1)} %add_rsqrt_fusion.1, f32[512]{0:T(512)S(1)} %broadcast_multiply_fusion.6), kind=kOutput, calls=%fused_computation.11 | convolution fusion | flops 2420244480 | bytes 9447424 | tf_op jit(solution)/shard_map/dot_general | solution.py:357
  167.3 6.4 %collective-permute-done.13 = bf16[512,256]{1,0:T(8,128)(2,1)S(1)} collective-permute-done((bf16[512,256]{1,0:T(8,128)(2,1)S(1)}, bf16[512,256]{1,0:T(8,128)(2,1)S(1)}, u32[]{:S(2)}, u32[]{:S(2)}) %collective-permute-start.13) | collective-permute-done | bytes 262176 | tf_op jit(solution)/shard_map/ppermute | solution.py:25
  175.6 38.7 %attend_back.1 = (bf16[2048,256]{1,0:T(8,128)(2,1)}, bf16[2048,384]{1,0:T(8,128)(2,1)}, bf16[2048,384]{1,0:T(8,128)(2,1)}, bf16[2048,384]{1,0:T(8,128)(2,1)}, bf...) custom-call(s32[256]{0:T(256)} %copy-done, s32[256]{0:T(256)} %reshape.493.live_ref, ...), custom_call_target="tpu_custom_call" | custom-call | flops 16106127360 | bytes 18874368 | tf_op jit(solution)/shard_map/attend_back/pallas_call | solution.py:238
  222.2 5.3 %collective-permute-start.38 = (bf16[64,768]{1,0:T(8,128)(2,1)S(1)}, bf16[64,768]{1,0:T(8,128)(2,1)S(1)}, u32[]{:S(2)}, u32[]{:S(2)}) collective-permute-start(bf16[64,768]{1,0:T(8,128)(2,1)S(1)} %get-tuple-element.91), channel_id=1, source_target_pairs={{16,0},{17,1},{18,2},{19,3},{20,4},{21,5},{22,6},{23,7},{24,8},{25... | collective-permute-start | bytes 294920 | tf_op jit(solution)/shard_map/ppermute | solution.py:31
  230.2 5.4 %collective-permute-start.40 = (bf16[64,768]{1,0:T(8,128)(2,1)S(1)}, bf16[64,768]{1,0:T(8,128)(2,1)S(1)}, u32[]{:S(2)}, u32[]{:S(2)}) collective-permute-start(bf16[64,768]{1,0:T(8,128)(2,1)S(1)} %get-tuple-element.89), channel_id=1, source_target_pairs={{24,0},{25,1},{26,2},{27,3},{28,4},{29,5},{30,6},{31,7}} | collective-permute-start | bytes 294920 | tf_op jit(solution)/shard_map/ppermute | solution.py:31
  255.1 26.8 %collective-permute-done.17 = bf16[2048,384]{1,0:T(8,128)(2,1)S(1)} collective-permute-done((bf16[2048,384]{1,0:T(8,128)(2,1)S(1)}, bf16[2048,384]{1,0:T(8,128)(2,1)S(1)}, u32[]{:S(2)}, u32[]{:S(2)}) %collective-permute-start.17) | collective-permute-done | bytes 1572896 | tf_op jit(solution)/shard_map/ppermute | solution.py:31
  304.1 5.4 %collective-permute-start.25 = (bf16[2,48,576]{2,1,0:T(8,128)(2,1)S(1)}, bf16[2,48,576]{2,1,0:T(8,128)(2,1)S(1)}, u32[]{:S(2)}, u32[]{:S(2)}) collective-permute-start(bf16[2,48,576]{2,1,0:T(8,128)(2,1)S(1)} %get-tuple-element.87), channel_id=1, source_target_pairs={{8,0},{9,1},{10,2},{11,3},{12,4},{13,5},{14,6},{15,7},{16,8},{17,9... | collective-permute-start | bytes 331784 | tf_op jit(solution)/shard_map/ppermute | solution.py:31
  310.8 5.5 %collective-permute-start.27 = (bf16[2,48,576]{2,1,0:T(8,128)(2,1)S(1)}, bf16[2,48,576]{2,1,0:T(8,128)(2,1)S(1)}, u32[]{:S(2)}, u32[]{:S(2)}) collective-permute-start(bf16[2,48,576]{2,1,0:T(8,128)(2,1)S(1)} %get-tuple-element.85), channel_id=1, source_target_pairs={{16,0},{17,1},{18,2},{19,3},{20,4},{21,5},{22,6},{23,7},{24,8},{25... | collective-permute-start | bytes 331784 | tf_op jit(solution)/shard_map/ppermute | solution.py:31
  317.5 6.4 %collective-permute-start.29 = (bf16[2,48,576]{2,1,0:T(8,128)(2,1)S(1)}, bf16[2,48,576]{2,1,0:T(8,128)(2,1)S(1)}, u32[]{:S(2)}, u32[]{:S(2)}) collective-permute-start(bf16[2,48,576]{2,1,0:T(8,128)(2,1)S(1)} %get-tuple-element.83), channel_id=1, source_target_pairs={{24,0},{25,1},{26,2},{27,3},{28,4},{29,5},{30,6},{31,7}} | collective-permute-start | bytes 331784 | tf_op jit(solution)/shard_map/ppermute | solution.py:31
  326.6 5.5 %collective-permute-start.47 = (bf16[48,3072]{1,0:T(8,128)(2,1)S(1)}, bf16[48,3072]{1,0:T(8,128)(2,1)S(1)}, u32[]{:S(2)}, u32[]{:S(2)}) collective-permute-start(bf16[48,3072]{1,0:T(8,128)(2,1)S(1)} %get-tuple-element.57), channel_id=1, source_target_pairs={{16,0},{17,1},{18,2},{19,3},{20,4},{21,5},{22,6},{23,7},{24,8},{25... | collective-permute-start | bytes 884744 | tf_op jit(solution)/shard_map/ppermute | solution.py:31
  333.4 6.4 %collective-permute-start.49 = (bf16[48,3072]{1,0:T(8,128)(2,1)S(1)}, bf16[48,3072]{1,0:T(8,128)(2,1)S(1)}, u32[]{:S(2)}, u32[]{:S(2)}) collective-permute-start(bf16[48,3072]{1,0:T(8,128)(2,1)S(1)} %get-tuple-element.55), channel_id=1, source_target_pairs={{24,0},{25,1},{26,2},{27,3},{28,4},{29,5},{30,6},{31,7}} | collective-permute-start | bytes 884744 | tf_op jit(solution)/shard_map/ppermute | solution.py:31
  364.3 5.5 %collective-permute-start.57 = (bf16[96,768]{1,0:T(8,128)(2,1)S(1)}, bf16[96,768]{1,0:T(8,128)(2,1)S(1)}, u32[]{:S(2)}, u32[]{:S(2)}) collective-permute-start(bf16[96,768]{1,0:T(8,128)(2,1)S(1)} %get-tuple-element.79), channel_id=1, source_target_pairs={{16,0},{17,1},{18,2},{19,3},{20,4},{21,5},{22,6},{23,7},{24,8},{25... | collective-permute-start | bytes 442376 | tf_op jit(solution)/shard_map/ppermute | solution.py:31
  376.1 6.4 %collective-permute-start.59 = (bf16[96,768]{1,0:T(8,128)(2,1)S(1)}, bf16[96,768]{1,0:T(8,128)(2,1)S(1)}, u32[]{:S(2)}, u32[]{:S(2)}) collective-permute-start(bf16[96,768]{1,0:T(8,128)(2,1)S(1)} %get-tuple-element.77), channel_id=1, source_target_pairs={{24,0},{25,1},{26,2},{27,3},{28,4},{29,5},{30,6},{31,7}} | collective-permute-start | bytes 442376 | tf_op jit(solution)/shard_map/ppermute | solution.py:31
  386.3 5.5 %collective-permute-done.20 = bf16[512,768]{1,0:T(8,128)(2,1)S(1)} collective-permute-done((bf16[512,768]{1,0:T(8,128)(2,1)S(1)}, bf16[512,768]{1,0:T(8,128)(2,1)S(1)}, u32[]{:S(2)}, u32[]{:S(2)}) %collective-permute-start.20) | collective-permute-done | bytes 786464 | tf_op jit(solution)/shard_map/ppermute | solution.py:25
  391.8 10.2 %collective-permute-done.21 = bf16[512,768]{1,0:T(8,128)(2,1)S(1)} collective-permute-done((bf16[512,768]{1,0:T(8,128)(2,1)S(1)}, bf16[512,768]{1,0:T(8,128)(2,1)S(1)}, u32[]{:S(2)}, u32[]{:S(2)}) %collective-permute-start.21) | collective-permute-done | bytes 786464 | tf_op jit(solution)/shard_map/ppermute | solution.py:25
  402.0 4.7 %collective-permute-done.22 = bf16[512,768]{1,0:T(8,128)(2,1)S(1)} collective-permute-done((bf16[512,768]{1,0:T(8,128)(2,1)S(1)}, bf16[512,768]{1,0:T(8,128)(2,1)S(1)}, u32[]{:S(2)}, u32[]{:S(2)}) %collective-permute-start.22) | collective-permute-done | bytes 786464 | tf_op jit(solution)/shard_map/ppermute | solution.py:25
  (315 shorter events, 155.7 us)
Async XLA Ops:
  0.6 20.7 %collective-permute-start.1 = (bf16[512,768]{1,0:T(8,128)(2,1)}, bf16[512,768]{1,0:T(8,128)(2,1)S(1)}, u32[]{:S(2)}, u32[]{:S(2)}) collective-permute-start(bf16[512,768]{1,0:T(8,128)(2,1)} %param.15), channel_id=1, source_target_pairs={{0,1},{1,0},{2,3},{3,2},{4,5},{5,4},{6,7},{7,6},{8,9},{9,8},{10,11... | collective-permute-start | bytes 2359304 | tf_op jit(solution)/shard_map/ppermute | solution.py:25
  2.2 36.1 %collective-permute-start.2 = (bf16[512,768]{1,0:T(8,128)(2,1)}, bf16[512,768]{1,0:T(8,128)(2,1)S(1)}, u32[]{:S(2)}, u32[]{:S(2)}) collective-permute-start(bf16[512,768]{1,0:T(8,128)(2,1)} %param.15), channel_id=1, source_target_pairs={{0,4},{1,5},{2,6},{3,7},{4,0},{5,1},{6,2},{7,3},{8,12},{9,13},{10,... | collective-permute-start | bytes 2359304 | tf_op jit(solution)/shard_map/ppermute | solution.py:25
  3.7 34.6 %collective-permute-start.3 = (bf16[512,768]{1,0:T(8,128)(2,1)}, bf16[512,768]{1,0:T(8,128)(2,1)S(1)}, u32[]{:S(2)}, u32[]{:S(2)}) collective-permute-start(bf16[512,768]{1,0:T(8,128)(2,1)} %param.15), channel_id=1, source_target_pairs={{0,5},{1,4},{2,7},{3,6},{4,1},{5,0},{6,3},{7,2},{8,13},{9,12},{10,... | collective-permute-start | bytes 2359304 | tf_op jit(solution)/shard_map/ppermute | solution.py:25
  4.2 45.6 %collective-permute-start = (s32[16,3]{0,1:T(4,128)}, s32[16,3]{0,1:T(4,128)S(1)}, u32[]{:S(2)}, u32[]{:S(2)}) collective-permute-start(s32[16,3]{0,1:T(4,128)} %param.29), channel_id=1, source_target_pairs={{0,4},{2,6},{4,0},{6,2},{8,12},{10,14},{12,8},{14,10},{16,20},{18,... | collective-permute-start | bytes 584 | tf_op jit(solution)/shard_map/ppermute | solution.py:311
  40.4 36.9 %collective-permute-start.4 = (bf16[2048,384]{1,0:T(8,128)(2,1)S(1)}, bf16[2048,384]{1,0:T(8,128)(2,1)S(1)}, u32[]{:S(2)}, u32[]{:S(2)}) collective-permute-start(bf16[2048,384]{1,0:T(8,128)(2,1)S(1)} %convolution_convert_fusion.2.refs_2_), channel_id=1, source_target_pairs={{0,8},{1,9},{2,10},{3,11},{4,12},{5,13},{6,14},{7,15},{8,16},{9,17... | collective-permute-start | bytes 4718600 | tf_op jit(solution)/shard_map/ppermute | solution.py:31
  41.7 36.7 %collective-permute-start.7 = (bf16[2048,384]{1,0:T(8,128)(2,1)S(1)}, bf16[2048,384]{1,0:T(8,128)(2,1)}, u32[]{:S(2)}, u32[]{:S(2)}) collective-permute-start(bf16[2048,384]{1,0:T(8,128)(2,1)S(1)} %convolution_convert_fusion.2.refs_2_), channel_id=1, source_target_pairs={{8,0},{9,1},{10,2},{11,3},{12,4},{13,5},{14,6},{15,7},{16,8},{17,9... | collective-permute-start | bytes 4718600 | tf_op jit(solution)/shard_map/ppermute | solution.py:31
  49.9 32.3 %collective-permute-start.6 = (bf16[2048,384]{1,0:T(8,128)(2,1)S(1)}, bf16[2048,384]{1,0:T(8,128)(2,1)}, u32[]{:S(2)}, u32[]{:S(2)}) collective-permute-start(bf16[2048,384]{1,0:T(8,128)(2,1)S(1)} %convolution_convert_fusion.2.refs_2_), channel_id=1, source_target_pairs={{0,2},{1,3},{2,0},{3,1},{4,6},{5,7},{6,4},{7,5},{8,10},{9,11},{10,... | collective-permute-start | bytes 4718600 | tf_op jit(solution)/shard_map/ppermute | solution.py:25
  158.0 16.8 %collective-permute-start.33 = (bf16[4,2,64,768]{3,2,1,0:T(8,128)(2,1)S(1)}, bf16[4,2,64,768]{3,2,1,0:T(8,128)(2,1)S(1)}, u32[]{:S(2)}, u32[]{:S(2)}) collective-permute-start(bf16[4,2,64,768]{3,2,1,0:T(8,128)(2,1)S(1)} %fusion.33), channel_id=1, source_target_pairs={{0,2},{1,3},{2,0},{3,1},{4,6},{5,7},{6,4},{7,5},{8,10},{9,11},{10,... | collective-permute-start | bytes 2359304 | tf_op jit(solution)/shard_map/ppermute | solution.py:25
  175.0 39.4 %collective-permute-start.34 = (bf16[4,64,768]{2,1,0:T(8,128)(2,1)S(1)}, bf16[4,64,768]{2,1,0:T(8,128)(2,1)S(1)}, u32[]{:S(2)}, u32[]{:S(2)}) collective-permute-start(bf16[4,64,768]{2,1,0:T(8,128)(2,1)S(1)} %dynamic-slice_bitcast_fusion.5), channel_id=1, source_target_pairs={{0,4},{1,5},{2,6},{3,7},{4,0},{5,1},{6,2},{7,3},{8,12},{9,13},{10,... | collective-permute-start | bytes 1179656 | tf_op jit(solution)/shard_map/ppermute | solution.py:25
  214.3 31.1 %collective-permute-start.16 = (bf16[2048,384]{1,0:T(8,128)(2,1)}, bf16[2048,384]{1,0:T(8,128)(2,1)S(1)}, u32[]{:S(2)}, u32[]{:S(2)}) collective-permute-start(bf16[2048,384]{1,0:T(8,128)(2,1)} %get-tuple-element.23), channel_id=1, source_target_pairs={{0,2},{1,3},{2,0},{3,1},{4,6},{5,7},{6,4},{7,5},{8,10},{9,11},{10,... | collective-permute-start | bytes 4718600 | tf_op jit(solution)/shard_map/ppermute | solution.py:25
  221.9 27.2 %collective-permute-start.51 = (bf16[4,2,192,768]{3,2,1,0:T(8,128)(2,1)S(1)}, bf16[4,2,192,768]{3,2,1,0:T(8,128)(2,1)S(1)}, u32[]{:S(2)}, u32[]{:S(2)}) collective-permute-start(bf16[4,2,192,768]{3,2,1,0:T(8,128)(2,1)S(1)} %dynamic-slice_bitcast_fusion), channel_id=1, source_target_pairs={{0,2},{1,3},{2,0},{3,1},{4,6},{5,7},{6,4},{7,5},{8,10},{9,11},{10,... | collective-permute-start | bytes 7077896 | tf_op jit(solution)/shard_map/ppermute | solution.py:25
  245.9 36.0 %collective-permute-start.17 = (bf16[2048,384]{1,0:T(8,128)(2,1)S(1)}, bf16[2048,384]{1,0:T(8,128)(2,1)S(1)}, u32[]{:S(2)}, u32[]{:S(2)}) collective-permute-start(bf16[2048,384]{1,0:T(8,128)(2,1)S(1)} %add_convert_fusion.2), channel_id=1, source_target_pairs={{8,0},{9,1},{10,2},{11,3},{12,4},{13,5},{14,6},{15,7},{16,8},{17,9... | collective-permute-start | bytes 4718600 | tf_op jit(solution)/shard_map/ppermute | solution.py:31
  247.8 38.7 %collective-permute-start.19 = (bf16[2048,384]{1,0:T(8,128)(2,1)S(1)}, bf16[2048,384]{1,0:T(8,128)(2,1)S(1)}, u32[]{:S(2)}, u32[]{:S(2)}) collective-permute-start(bf16[2048,384]{1,0:T(8,128)(2,1)S(1)} %add_convert_fusion.1), channel_id=1, source_target_pairs={{0,8},{1,9},{2,10},{3,11},{4,12},{5,13},{6,14},{7,15},{8,16},{9,17... | collective-permute-start | bytes 4718600 | tf_op jit(solution)/shard_map/ppermute | solution.py:31
  251.0 51.6 %collective-permute-start.52 = (bf16[4,2,96,768]{3,2,1,0:T(8,128)(2,1)}, bf16[4,2,96,768]{3,2,1,0:T(8,128)(2,1)}, u32[]{:S(2)}, u32[]{:S(2)}) collective-permute-start(bf16[4,2,96,768]{3,2,1,0:T(8,128)(2,1)} %dynamic-slice_bitcast_fusion.1), channel_id=1, source_target_pairs={{0,1},{1,0},{2,3},{3,2},{4,5},{5,4},{6,7},{7,6},{8,9},{9,8},{10,11... | collective-permute-start | bytes 3538952 | tf_op jit(solution)/shard_map/ppermute | solution.py:25
  253.9 42.5 %collective-permute-start.43 = (bf16[4,48,3072]{2,1,0:T(8,128)(2,1)}, bf16[4,48,3072]{2,1,0:T(8,128)(2,1)}, u32[]{:S(2)}, u32[]{:S(2)}) collective-permute-start(bf16[4,48,3072]{2,1,0:T(8,128)(2,1)} %dynamic-slice_bitcast_fusion.2), channel_id=1, source_target_pairs={{0,4},{1,5},{2,6},{3,7},{4,0},{5,1},{6,2},{7,3},{8,12},{9,13},{10,... | collective-permute-start | bytes 3538952 | tf_op jit(solution)/shard_map/ppermute | solution.py:25
  304.1 19.9 %collective-permute-start.25 = (bf16[2,48,576]{2,1,0:T(8,128)(2,1)S(1)}, bf16[2,48,576]{2,1,0:T(8,128)(2,1)S(1)}, u32[]{:S(2)}, u32[]{:S(2)}) collective-permute-start(bf16[2,48,576]{2,1,0:T(8,128)(2,1)S(1)} %get-tuple-element.87), channel_id=1, source_target_pairs={{8,0},{9,1},{10,2},{11,3},{12,4},{13,5},{14,6},{15,7},{16,8},{17,9... | collective-permute-start | bytes 331784 | tf_op jit(solution)/shard_map/ppermute | solution.py:31
  325.3 19.6 %collective-permute-start.46 = (bf16[48,3072]{1,0:T(8,128)(2,1)S(1)}, bf16[48,3072]{1,0:T(8,128)(2,1)S(1)}, u32[]{:S(2)}, u32[]{:S(2)}) collective-permute-start(bf16[48,3072]{1,0:T(8,128)(2,1)S(1)} %get-tuple-element.58), channel_id=1, source_target_pairs={{0,16},{1,17},{2,18},{3,19},{4,20},{5,21},{6,22},{7,23},{8,24},{9,... | collective-permute-start | bytes 884744 | tf_op jit(solution)/shard_map/ppermute | solution.py:31
  326.6 19.3 %collective-permute-start.47 = (bf16[48,3072]{1,0:T(8,128)(2,1)S(1)}, bf16[48,3072]{1,0:T(8,128)(2,1)S(1)}, u32[]{:S(2)}, u32[]{:S(2)}) collective-permute-start(bf16[48,3072]{1,0:T(8,128)(2,1)S(1)} %get-tuple-element.57), channel_id=1, source_target_pairs={{16,0},{17,1},{18,2},{19,3},{20,4},{21,5},{22,6},{23,7},{24,8},{25... | collective-permute-start | bytes 884744 | tf_op jit(solution)/shard_map/ppermute | solution.py:31
  340.0 16.8 %collective-permute-start.53 = (bf16[4,96,768]{2,1,0:T(8,128)(2,1)S(1)}, bf16[4,96,768]{2,1,0:T(8,128)(2,1)S(1)}, u32[]{:S(2)}, u32[]{:S(2)}) collective-permute-start(bf16[4,96,768]{2,1,0:T(8,128)(2,1)S(1)} %dynamic-slice_bitcast_fusion.3), channel_id=1, source_target_pairs={{0,4},{1,5},{2,6},{3,7},{4,0},{5,1},{6,2},{7,3},{8,12},{9,13},{10,... | collective-permute-start | bytes 1769480 | tf_op jit(solution)/shard_map/ppermute | solution.py:25
  348.6 22.7 %collective-permute-start.50 = (bf16[48,3072]{1,0:T(8,128)(2,1)S(1)}, bf16[48,3072]{1,0:T(8,128)(2,1)S(1)}, u32[]{:S(2)}, u32[]{:S(2)}) collective-permute-start(bf16[48,3072]{1,0:T(8,128)(2,1)S(1)} %fusion.42), channel_id=1, source_target_pairs={{0,1},{1,0},{2,3},{3,2},{4,5},{5,4},{6,7},{7,6},{8,9},{9,8},{10,11... | collective-permute-start | bytes 884744 | tf_op jit(solution)/shard_map/ppermute | solution.py:25
  371.3 20.5 %collective-permute-start.20 = (bf16[512,768]{1,0:T(8,128)(2,1)S(1)}, bf16[512,768]{1,0:T(8,128)(2,1)S(1)}, u32[]{:S(2)}, u32[]{:S(2)}) collective-permute-start(bf16[512,768]{1,0:T(8,128)(2,1)S(1)} %get-tuple-element.50), channel_id=1, source_target_pairs={{0,1},{1,0},{2,3},{3,2},{4,5},{5,4},{6,7},{7,6},{8,9},{9,8},{10,11... | collective-permute-start | bytes 2359304 | tf_op jit(solution)/shard_map/ppermute | solution.py:25
  372.2 29.7 %collective-permute-start.21 = (bf16[512,768]{1,0:T(8,128)(2,1)S(1)}, bf16[512,768]{1,0:T(8,128)(2,1)S(1)}, u32[]{:S(2)}, u32[]{:S(2)}) collective-permute-start(bf16[512,768]{1,0:T(8,128)(2,1)S(1)} %get-tuple-element.52), channel_id=1, source_target_pairs={{0,4},{1,5},{2,6},{3,7},{4,0},{5,1},{6,2},{7,3},{8,12},{9,13},{10,... | collective-permute-start | bytes 2359304 | tf_op jit(solution)/shard_map/ppermute | solution.py:25
  373.4 33.3 %collective-permute-start.22 = (bf16[512,768]{1,0:T(8,128)(2,1)S(1)}, bf16[512,768]{1,0:T(8,128)(2,1)S(1)}, u32[]{:S(2)}, u32[]{:S(2)}) collective-permute-start(bf16[512,768]{1,0:T(8,128)(2,1)S(1)} %get-tuple-element.51), channel_id=1, source_target_pairs={{0,5},{1,4},{2,7},{3,6},{4,1},{5,0},{6,3},{7,2},{8,13},{9,12},{10,... | collective-permute-start | bytes 2359304 | tf_op jit(solution)/shard_map/ppermute | solution.py:25
  385.3 23.0 %collective-permute-start.60 = (bf16[96,768]{1,0:T(8,128)(2,1)S(1)}, bf16[96,768]{1,0:T(8,128)(2,1)S(1)}, u32[]{:S(2)}, u32[]{:S(2)}) collective-permute-start(bf16[96,768]{1,0:T(8,128)(2,1)S(1)} %fusion.57), channel_id=1, source_target_pairs={{0,1},{1,0},{2,3},{3,2},{4,5},{5,4},{6,7},{7,6},{8,9},{9,8},{10,11... | collective-permute-start | bytes 442376 | tf_op jit(solution)/shard_map/ppermute | solution.py:25
  (79 other events, 872.8 us)

commit v2 on v1

--- a/solution.py
+++ b/solution.py
@@ -105,12 +105,10 @@
     return total
 
 
-def fetch(pieces, kv, sems):
-    rows = pieces[0].shape[0]
-    for n, piece in enumerate(pieces):
-        pltpu.make_async_copy(piece, kv.at[pl.ds(n * rows, rows)], sems.at[n]).start()
-    for n, piece in enumerate(pieces):
-        pltpu.make_async_copy(piece, kv.at[pl.ds(n * rows, rows)], sems.at[n]).wait()
+def fetch(source, kv, sems):
+    copy = pltpu.make_async_copy(source, kv, sems.at[0])
+    copy.start()
+    copy.wait()
 
 
 def nt(a, b):
@@ -122,8 +120,8 @@
 
 
 def forward_kernel(idx_ref, bias_ref, q_ref, *refs):
-    pieces, ctx_ref, kv, sems = refs[:6], refs[6], refs[7], refs[8]
-    fetch(pieces, kv, sems)
+    kv_ref, ctx_ref, kv, sems = refs
+    fetch(kv_ref, kv, sems)
 
     def step(i, carry):
         q_rows = pl.multiple_of(i * BLK, BLK)
@@ -145,19 +143,16 @@
 
 
 def backward_kernel(idx_ref, live_ref, q_ref, do_ref, *refs):
-    pieces, dq_ref, outs = refs[:6], refs[6], refs[7:13]
-    kv, acc, sems = refs[13:]
-    rows_piece = pieces[0].shape[0]
+    kv_ref, dq_ref, dkv_ref, kv, acc, sems = refs
 
     def clear(n, carry):
         acc[pl.ds(pl.multiple_of(n * 256, 256), 256), :] = jnp.zeros((256, 2 * WQ), jnp.float32)
         return carry
 
-    for n, piece in enumerate(pieces):
-        pltpu.make_async_copy(piece, kv.at[pl.ds(n * rows_piece, rows_piece)], sems.at[n]).start()
+    copy = pltpu.make_async_copy(kv_ref, kv, sems.at[0])
+    copy.start()
     lax.fori_loop(0, acc.shape[0] // 256, clear, 0)
-    for n, piece in enumerate(pieces):
-        pltpu.make_async_copy(piece, kv.at[pl.ds(n * rows_piece, rows_piece)], sems.at[n]).wait()
+    copy.wait()
 
     def step(i, carry):
         q_rows = pl.multiple_of(i * BLK, BLK)
@@ -197,13 +192,11 @@
     lax.fori_loop(0, q_ref.shape[0] // BLK, step, 0)
 
     def emit(n, carry):
-        at = pl.multiple_of(n * 256, 256)
-        for j in range(6):
-            part = acc[pl.ds(j * rows_piece + at, 256), :]
-            outs[j][pl.ds(at, 256), :] = part.astype(jnp.bfloat16)
+        at = pl.ds(pl.multiple_of(n * 256, 256), 256)
+        dkv_ref[at, :] = acc[at, :].astype(jnp.bfloat16)
         return carry
 
-    lax.fori_loop(0, rows_piece // 256, emit, 0)
+    lax.fori_loop(0, acc.shape[0] // 256, emit, 0)
 
 
 VMEM = pl.BlockSpec(memory_space=pltpu.VMEM)
@@ -211,46 +204,514 @@
 ANY = pl.BlockSpec(memory_space=pl.ANY)
 
 
-def attend(idx, bias, queries, pieces):
-    rows, width = pieces[0].shape
+def device_at(plane, y_at, core, x_at):
+    return (plane * 4 + y_at * 2 + core, x_at)
+
+
+def place():
+    seq_at, x_at = lax.axis_index("seq"), lax.axis_index("head")
+    return seq_at // 4, (seq_at // 2) % 2, seq_at % 2, x_at
+
+
+def remote(src, dst, sems, recvs, at, device):
+    return pltpu.make_async_remote_copy(
+        src_ref=src,
+        dst_ref=dst,
+        send_sem=sems.at[at],
+        recv_sem=recvs.at[at],
+        device_id=device,
+        device_id_type=pl.DeviceIdType.MESH,
+    )
+
+
+def greet(partners):
+    barrier = pltpu.get_barrier_semaphore()
+    for device in partners:
+        pl.semaphore_signal(
+            barrier, inc=1, device_id=device, device_id_type=pl.DeviceIdType.MESH
+        )
+    pl.semaphore_wait(barrier, len(partners))
+
+
+CHUNK_ORDER = (0, 1, 2, 4, 3, 5, 6, 7)
+
+
+def gather_kernel(planes, tok_ref, wq_ref, wkv_ref, kv_out, q_ref, x_out, xs, kvs, *sems):
+    x_send, x_recv, k_send, k_recv, up_send, up_recv, dn_send, dn_recv = sems[:8]
+    f_send, f_recv, g_send, g_recv, l_sem, s_sem = sems[8:]
+    plane, y_at, core, x_at = place()
+    piece = tok_ref.shape[0]
+    rows = piece // 2
+    part = 4 * piece
+    by_x = device_at(plane, y_at, core, 1 - x_at)
+    by_y = device_at(plane, 1 - y_at, core, x_at)
+    by_core = device_at(plane, y_at, 1 - core, x_at)
+    above = device_at(plane + 1, y_at, core, x_at)
+    below = device_at(plane - 1, y_at, core, x_at)
+    has_above, has_below = plane < planes - 1, plane > 0
+    ring = [device_at(lax.rem(plane + g, planes), y_at, core, x_at) for g in (1, planes - 1)]
+    greet([by_x, by_y, by_core] + ring)
+
+    def x_rows(c):
+        return xs.at[pl.ds((c - 2) * rows, rows)]
+
+    def tok_rows(c):
+        return tok_ref.at[pl.ds(c * rows, rows)]
+
+    hops = {
+        2: remote(tok_rows(0), x_rows(2), x_send, x_recv, 0, by_x),
+        4: remote(tok_rows(0), x_rows(4), x_send, x_recv, 2, by_y),
+        3: remote(tok_rows(1), x_rows(3), x_send, x_recv, 1, by_x),
+        5: remote(tok_rows(1), x_rows(5), x_send, x_recv, 3, by_y),
+        6: remote(x_rows(2), x_rows(6), x_send, x_recv, 4, by_y),
+        7: remote(x_rows(5), x_rows(7), x_send, x_recv, 5, by_x),
+    }
+    for c in (2, 4, 3, 5):
+        hops[c].start()
+
+    def kv_rows(part_at, c):
+        return kv_out.at[pl.ds(part_at * part + c * rows, rows)]
+
+    to_core, to_above, to_below, pass_up, pass_down = {}, {}, {}, {}, {}
+    stores = {}
+    for c in range(8):
+        mine = kvs.at[pl.ds(c * rows, rows)]
+        to_core[c] = remote(mine, kv_rows(3, c), k_send, k_recv, c, by_core)
+        to_above[c] = remote(mine, kv_rows(0, c), up_send, up_recv, c, above)
+        to_below[c] = remote(mine, kv_rows(4, c), dn_send, dn_recv, c, below)
+        pass_up[c] = remote(kv_rows(0, c), kv_rows(1, c), f_send, f_recv, c, by_core)
+        pass_down[c] = remote(kv_rows(4, c), kv_rows(5, c), g_send, g_recv, c, by_core)
+        stores[c] = pltpu.make_async_copy(mine, kv_rows(2, c), l_sem.at[c])
+    keeps = {
+        c: pltpu.make_async_copy(
+            tok_rows(c) if c < 2 else x_rows(c), x_out.at[pl.ds(c * rows, rows)], s_sem.at[c]
+        )
+        for c in range(8)
+    }
+
+    def relay(c):
+        @pl.when(has_below)
+        def _():
+            to_above[c].wait_recv()
+            pass_up[c].start()
+
+        @pl.when(has_above)
+        def _():
+            to_below[c].wait_recv()
+            pass_down[c].start()
+
+    for n, c in enumerate(CHUNK_ORDER):
+        if c >= 2:
+            hops[c].wait_recv()
+        if c == 2:
+            hops[6].start()
+        if c == 5:
+            hops[7].start()
+        keeps[c].start()
+        block = tok_ref[pl.ds(c * rows, rows), :] if c < 2 else xs[pl.ds((c - 2) * rows, rows), :]
+        kvs[pl.ds(c * rows, rows), :] = jnp.dot(
+            block, wkv_ref[...], preferred_element_type=jnp.float32
+        ).astype(jnp.bfloat16)
+
+        @pl.when(has_above)
+        def _(c=c):
+            to_above[c].start()
+
+        @pl.when(has_below)
+        def _(c=c):
+            to_below[c].start()
+
+        to_core[c].start()
+        stores[c].start()
+        q_ref[pl.ds(c * rows, rows), :] = jnp.dot(
+            block, wq_ref[...], preferred_element_type=jnp.float32
+        ).astype(jnp.bfloat16)
+        if n >= 3:
+            relay(CHUNK_ORDER[n - 3])
+    for c in CHUNK_ORDER[5:]:
+        relay(c)
+    for c in (2, 4, 3, 5, 6, 7):
+        hops[c].wait_send()
+    for c in range(8):
+        to_core[c].wait()
+        stores[c].wait()
+        keeps[c].wait()
+
+        @pl.when(has_above)
+        def _(c=c):
+            to_above[c].wait_send()
+            pass_down[c].wait()
+
+        @pl.when(has_below)
+        def _(c=c):
+            to_below[c].wait_send()
+            pass_up[c].wait()
+
+
+def gather_project(tokens, wq_own, wkv_own, planes):
+    piece, width = tokens.shape
+    dma = pltpu.SemaphoreType.DMA
+    return pl.pallas_call(
+        functools.partial(gather_kernel, planes),
+        out_shape=[
+            jax.ShapeDtypeStruct((24 * piece, 2 * WQ), jnp.bfloat16),
+            jax.ShapeDtypeStruct((4 * piece, WIN), jnp.bfloat16),
+            jax.ShapeDtypeStruct((4 * piece, width), jnp.bfloat16),
+        ],
+        in_specs=[VMEM] * 3,
+        out_specs=[ANY, VMEM, ANY],
+        scratch_shapes=[
+            pltpu.VMEM((3 * piece, width), jnp.bfloat16),
+            pltpu.VMEM((4 * piece, 2 * WQ), jnp.bfloat16),
+            dma((6,)),
+            dma((6,)),
+        ]
+        + [dma((8,))] * 12,
+        compiler_params=pltpu.CompilerParams(
+            collective_id=0, has_side_effects=True, vmem_limit_bytes=20 << 20
+        ),
+        cost_estimate=pl.CostEstimate(
+            flops=2 * 4 * piece * width * 640, bytes_accessed=40 << 20, transcendentals=0
+        ),
+        name="gather_project",
+    )(tokens, wq_own, wkv_own)
+
+
+def attend(idx, bias, queries, keys_values):
+    rows, width = keys_values.shape[0] // 6, keys_values.shape[1]
     count = queries.shape[0]
     return pl.pallas_call(
         forward_kernel,
         out_shape=jax.ShapeDtypeStruct((count, WIN), jnp.bfloat16),
-        in_specs=[SMEM, VMEM, VMEM] + [ANY] * 6,
+        in_specs=[SMEM, VMEM, VMEM] + [ANY],
         out_specs=VMEM,
         scratch_shapes=[
             pltpu.VMEM((6 * rows, width), jnp.bfloat16),
-            pltpu.SemaphoreType.DMA((6,)),
+            pltpu.SemaphoreType.DMA((1,)),
         ],
         compiler_params=pltpu.CompilerParams(vmem_limit_bytes=24 << 20),
         cost_estimate=pl.CostEstimate(
             flops=2 * 4 * count * 3 * 256 * 512, bytes_accessed=12 * rows * width, transcendentals=count * 3 * 512
         ),
         name="attend",
-    )(idx, bias, queries, *pieces)
-
-
-def attend_back(idx, live, queries, grads, pieces):
-    rows, width = pieces[0].shape
+    )(idx, bias, queries, keys_values)
+
+
+def attend_back(idx, live, queries, grads, keys_values):
+    rows, width = keys_values.shape[0] // 6, keys_values.shape[1]
     count = queries.shape[0]
-    kv_shape = jax.ShapeDtypeStruct((rows, width), jnp.bfloat16)
+    kv_shape = jax.ShapeDtypeStruct((6 * rows, width), jnp.bfloat16)
     return pl.pallas_call(
         backward_kernel,
-        out_shape=[jax.ShapeDtypeStruct((count, WIN), jnp.bfloat16)] + [kv_shape] * 6,
-        in_specs=[SMEM, SMEM, VMEM, VMEM] + [ANY] * 6,
-        out_specs=[VMEM] * 7,
+        out_shape=[jax.ShapeDtypeStruct((count, WIN), jnp.bfloat16)] + [kv_shape],
+        in_specs=[SMEM, SMEM, VMEM, VMEM] + [ANY],
+        out_specs=[VMEM] * 2,
         scratch_shapes=[
             pltpu.VMEM((6 * rows, width), jnp.bfloat16),
             pltpu.VMEM((6 * rows, width), jnp.float32),
-            pltpu.SemaphoreType.DMA((6,)),
+            pltpu.SemaphoreType.DMA((1,)),
         ],
         compiler_params=pltpu.CompilerParams(vmem_limit_bytes=56 << 20),
         cost_estimate=pl.CostEstimate(
             flops=2 * 10 * count * 3 * 256 * 512, bytes_accessed=24 * rows * width, transcendentals=count * 3 * 512
         ),
         name="attend_back",
-    )(idx, live, queries, grads, *pieces)
+    )(idx, live, queries, grads, keys_values)
+
+
+JORDER = (3, 1, 2, 0)
+
+
+def reduce_kernel(planes, n_own, *refs):
+    (dkv_in, dq_ref, x_ref, wq_ref, wkv_ref, up_a, up_b, out_a, out_b, down_a, down_b) = refs[:11]
+    attn_out, proj_out, up_out, down_out, side_out = refs[11:16]
+    (own, core_in, z_out, z_in, g_all, dx_out, dx_in, acc) = refs[16:24]
+    (p_slab, p_core, p_z, p_zin, p_fin) = refs[24:29]
+    w_sum, w_got, w_two, w_zin = refs[29:32], refs[32:35], refs[35:38], refs[38:41]
+    (l_sem, c_s, c_r, u_s, u_r, d_s, d_r, x_s, x_r) = refs[41:50]
+    (pk_s, pk_r, pz_s, pz_r, pf_s, pf_r) = refs[50:56]
+    (w2_s, w2_r, w3_s, w3_r, w4_s, w4_r) = refs[56:62]
+    plane, y_at, core, x_at = place()
+    piece = attn_out.shape[0]
+    part = 4 * piece
+    rest = planes - 1
+
+    def there(j):
+        return device_at(plane, y_at ^ (j >> 1), core, x_at ^ (j & 1))
+
+    by_x, by_y, by_xy = there(1), there(2), there(3)
+    by_core = device_at(plane, y_at, 1 - core, x_at)
+    others = [device_at(lax.rem(plane + g, planes), y_at, core, x_at) for g in range(1, planes)]
+
+    greet([by_x, by_y, by_xy, by_core] + others)
+
+    has_above, has_below = plane < planes - 1, plane > 0
+    above = device_at(plane + 1, y_at, core, x_at)
+    below = device_at(plane - 1, y_at, core, x_at)
+
+    def rows(r, j):
+        return pl.ds(r * part + j * piece, piece)
+
+    def in_rows(r, kk, j):
+        return pl.ds((2 * r + kk) * part + j * piece, piece)
+
+    turns = [(r, j) for j in JORDER for r in (0, 2)] + [(1, j) for j in JORDER]
+    loads, to_core = {}, {}
+    for n, (r, j) in enumerate(turns):
+        loads[r, j] = pltpu.make_async_copy(
+            dkv_in.at[in_rows(r, 0, j)], own.at[rows(r, j)], l_sem.at[n]
+        )
+        to_core[r, j] = remote(
+            dkv_in.at[in_rows(r, 1, j)], core_in.at[rows(r, j)], c_s, c_r, n, by_core
+        )
+    for key in turns:
+        to_core[key].start()
+        loads[key].start()
+
+    halves = [up_a.shape[2] // 2, out_a.shape[2] // 2]
+    pairs = [(up_a, up_b), (out_a, out_b)]
+    w2 = []
+    for n in range(2):
+        a, b = pairs[n]
+        for p in range(planes):
+            w_sum[n][p] = (a[p].astype(jnp.float32) + b[p].astype(jnp.float32)).astype(jnp.bfloat16)
+        give = pl.ds(pl.multiple_of((1 - x_at) * halves[n], 128), halves[n])
+        w2.append(remote(w_sum[n].at[:, :, give], w_got[n], w2_s, w2_r, n, by_x))
+        w2[n].start()
+    for p in range(planes):
+        for y in range(2):
+            w_sum[2][p, y] = (
+                down_a[p, y].astype(jnp.float32) + down_b[p, y].astype(jnp.float32)
+            ).astype(jnp.bfloat16)
+    w2.append(remote(w_sum[2].at[:, 1 - y_at], w_got[2], w2_s, w2_r, 2, by_y))
+    w2[2].start()
+
+    to_below, to_above = {}, {}
+    for n, j in enumerate(JORDER):
+        to_below[j] = remote(
+            z_out.at[rows(0, j)], z_in.at[rows(0, j)], d_s, d_r, n, below
+        )
+        to_above[j] = remote(
+            z_out.at[rows(1, j)], z_in.at[rows(1, j)], u_s, u_r, n, above
+        )
+
+    def both(r, j):
+        to_core[r, j].wait_recv()
+        loads[r, j].wait()
+        at = rows(r, j)
+        return own[at, :].astype(jnp.float32) + core_in[at, :].astype(jnp.float32)
+
+    for j in JORDER:
+        z_out[rows(0, j), :] = both(0, j).astype(jnp.bfloat16)
+
+        @pl.when(has_below)
+        def _(j=j):
+            to_below[j].start()
+
+        z_out[rows(1, j), :] = both(2, j).astype(jnp.bfloat16)
+
+        @pl.when(has_above)
+        def _(j=j):
+            to_above[j].start()
+
+    w3 = []
+    for n in range(3):
+        w2[n].wait_recv()
+        for p in range(planes):
+            if n < 2:
+                keep = w_sum[n][p, :, pl.ds(pl.multiple_of(x_at * halves[n], 128), halves[n])]
+            else:
+                keep = w_sum[n][p, y_at]
+            w_two[n][p] = (
+                keep.astype(jnp.float32) + w_got[n][p].astype(jnp.float32)
+            ).astype(jnp.bfloat16)
+        for g in range(1, planes):
+            w3.append(
+                remote(
+                    w_two[n].at[lax.rem(plane + g, planes)],
+                    w_zin[n].at[g - 1],
+                    w3_s,
+                    w3_r,
+                    n * rest + g - 1,
+                    others[g - 1],
+                )
+            )
+            w3[-1].start()
+
+    to_owner = {
+        j: remote(
+            dx_out.at[pl.ds((j - 1) * piece, piece)],
+            dx_in.at[pl.ds((j - 1) * piece, piece)],
+            x_s,
+            x_r,
+            j - 1,
+            there(j),
+        )
+        for j in (1, 2, 3)
+    }
+    first = True
+    for j in JORDER:
+        g_all[:, 2 * WQ :] = dq_ref[pl.ds(j * piece, piece), :]
+        g_all[:, : 2 * WQ] = both(1, j).astype(jnp.bfloat16)
+
+        @pl.when(has_above)
+        def _(j=j):
+            to_below[j].wait_recv()
+            g_all[:, : 2 * WQ] = (
+                g_all[:, : 2 * WQ].astype(jnp.float32) + z_in[rows(0, j), :].astype(jnp.float32)
+            ).astype(jnp.bfloat16)
+
+        @pl.when(has_below)
+        def _(j=j):
+            to_above[j].wait_recv()
+            g_all[:, : 2 * WQ] = (
+                g_all[:, : 2 * WQ].astype(jnp.float32) + z_in[rows(1, j), :].astype(jnp.float32)
+            ).astype(jnp.bfloat16)
+
+        grads = g_all[...]
+        dx = nt(grads[:, 2 * WQ :], wq_ref[...]) + nt(grads[:, : 2 * WQ], wkv_ref[...])
+        if j:
+            dx_out[pl.ds((j - 1) * piece, piece), :] = dx.astype(jnp.bfloat16)
+            to_owner[j].start()
+        else:
+            attn_out[...] = dx
+        step = tn(x_ref[pl.ds(j * piece, piece), :], grads)
+        acc[...] = step if first else acc[...] + step
+        first = False
+
+    share = p_slab.shape[3]
+    for p in range(planes):
+        for y in range(2):
+            for k in range(2):
+                at = ((p * 2 + y) * 2 + k) * share
+                p_slab[k, p, y] = acc[at : at + share, :].astype(jnp.bfloat16)
+    pk = remote(p_slab.at[1 - core], p_core, pk_s, pk_r, 0, by_core)
+    pk.start()
+
+    outs = [up_out, side_out, down_out]
+    w4 = []
+    for n in range(3):
+        total = w_two[n][plane].astype(jnp.float32)
+        for g in range(1, planes):
+            w3[n * rest + g - 1].wait_recv()
+            total = total + w_zin[n][g - 1].astype(jnp.float32)
+        outs[n][x_at] = total.astype(jnp.bfloat16)
+        w4.append(remote(outs[n].at[x_at], outs[n].at[x_at], w4_s, w4_r, n, by_x))
+        w4[n].start()
+
+    pk.wait_recv()
+    for p in range(planes):
+        p_z[p] = (
+            p_slab[core, p].astype(jnp.float32) + p_core[p].astype(jnp.float32)
+        ).astype(jnp.bfloat16)
+    pz = []
+    for g in range(1, planes):
+        pz.append(
+            remote(
+                p_z.at[lax.rem(plane + g, planes)], p_zin.at[g - 1], pz_s, pz_r, g - 1, others[g - 1]
+            )
+        )
+        pz[-1].start()
+
+    total = attn_out[...]
+    for j in (3, 1, 2):
+        to_owner[j].wait_recv()
+        total = total + dx_in[pl.ds((j - 1) * piece, piece), :].astype(jnp.float32)
+    attn_out[...] = total
+
+    total = p_z[plane].astype(jnp.float32)
+    for g in range(1, planes):
+        pz[g - 1].wait_recv()
+        total = total + p_zin[g - 1].astype(jnp.float32)
+    p_fin[...] = total.astype(jnp.bfloat16)
+    pf = []
+    for j in (1, 2, 3):
+        pf.append(
+            remote(p_fin.at[y_at ^ (j >> 1)], proj_out.at[j], pf_s, pf_r, j - 1, there(j))
+        )
+        pf[-1].start()
+    proj_out[0] = p_fin[y_at]
+    for copy in pf:
+        copy.wait()
+    for copy in w4:
+        copy.wait()
+    for copy in w2 + w3 + pz + [pk]:
+        copy.wait_send()
+    for key in turns:
+        to_core[key].wait_send()
+    for j in (1, 2, 3):
+        to_owner[j].wait_send()
+    for j in JORDER:
+
+        @pl.when(has_below)
+        def _(j=j):
+            to_below[j].wait_send()
+
+        @pl.when(has_above)
+        def _(j=j):
+            to_above[j].wait_send()
+
+
+def reduce_all(dkv, dq, stretch, wq, wkv, up, out, down, planes):
+    low = jnp.bfloat16
+    piece = dq.shape[0] // 4
+    width = stretch.shape[1]
+    share = up[0].shape[1]
+    rest = planes - 1
+    dma = pltpu.SemaphoreType.DMA
+    vm = pltpu.VMEM
+    side = out[0].shape[1]
+    kinds = [(share, up[0].shape[2] // 2), (side, width // 2), (down[0].shape[2], down[0].shape[3])]
+    cols = 2 * WQ + WIN
+    sds = jax.ShapeDtypeStruct
+    return pl.pallas_call(
+        functools.partial(reduce_kernel, planes, 0),
+        out_shape=[
+            sds((piece, width), jnp.float32),
+            sds((4, share, cols), low),
+            sds((2,) + kinds[0], low),
+            sds((2,) + kinds[2], low),
+            sds((2,) + kinds[1], low),
+        ],
+        in_specs=[ANY] + [VMEM] * 10,
+        out_specs=[VMEM] * 5,
+        scratch_shapes=[
+            vm((12 * piece, 2 * WQ), low),
+            vm((12 * piece, 2 * WQ), low),
+            vm((8 * piece, 2 * WQ), low),
+            vm((8 * piece, 2 * WQ), low),
+            vm((piece, cols), low),
+            vm((3 * piece, width), low),
+            vm((3 * piece, width), low),
+            vm((width, cols), jnp.float32),
+            vm((2, planes, 2, share, cols), low),
+            vm((planes, 2, share, cols), low),
+            vm((planes, 2, share, cols), low),
+            vm((rest, 2, share, cols), low),
+            vm((2, share, cols), low),
+            vm(up[0].shape, low),
+            vm(out[0].shape, low),
+            vm(down[0].shape, low),
+        ]
+        + [vm((planes,) + k, low) for k in kinds] * 2
+        + [vm((rest,) + k, low) for k in kinds]
+        + [dma((12,))] * 3
+        + [dma((4,))] * 4
+        + [dma((3,))] * 2
+        + [dma((1,))] * 2
+        + [dma((rest,))] * 2
+        + [dma((3,))] * 2
+        + [dma((3,))] * 2
+        + [dma((3 * rest,))] * 2
+        + [dma((3,))] * 2,
+        compiler_params=pltpu.CompilerParams(
+            collective_id=1, has_side_effects=True, vmem_limit_bytes=58 << 20
+        ),
+        cost_estimate=pl.CostEstimate(
+            flops=4 * 4 * piece * width * cols, bytes_accessed=40 << 20, transcendentals=0
+        ),
+        name="reduce_all",
+    )(dkv, dq, stretch, wq, wkv, up[0], up[1], out[0], out[1], down[0], down[1])
 
 
 def add_low(*terms):
@@ -305,9 +766,6 @@
     plane, y_at, core = seq_at // 4, (seq_at // 2) % 2, seq_at % 2
     group = y_at * 2 + x_at
 
-    from_x = xor_swap(tokens, 1)
-    from_y = xor_swap(tokens, 4)
-    from_xy = xor_swap(tokens, 5)
     rand_y = lax.ppermute(rand_blocks, "seq", [(s, s ^ 2) for s in range(seqs)])
 
     def columns(weights):
@@ -356,20 +814,8 @@
     def low_dot(a, b):
         return jnp.dot(a, b, preferred_element_type=jnp.float32).astype(jnp.bfloat16)
 
-    stretch = jnp.concatenate([tokens, from_x, from_y, from_xy], axis=0)
-    kv_own = low_dot(stretch, wkv_own)
-    queries = low_dot(stretch, wq_own)
-    kv_below = plane_shift(kv_own, 1)
-    kv_above = plane_shift(kv_own, -1)
-    pieces = [
-        kv_below,
-        xor_swap(kv_below, 2),
-        kv_own,
-        xor_swap(kv_own, 2),
-        kv_above,
-        xor_swap(kv_above, 2),
-    ]
-    context = attend(idx, bias, queries, pieces)
+    keys_values, queries, stretch = gather_project(tokens, wq_own, wkv_own, planes)
+    context = attend(idx, bias, queries, keys_values)
 
     def to_owners(array):
         parts = array.reshape(4, piece, -1)
@@ -416,63 +862,40 @@
     up_slabs = grad_w_up.reshape(seqs, share, -1)
     down_slabs = grad_w_down.reshape(seqs, -1, width)
 
-    def y_then_x(slabs):
+    def y_first(slabs):
         slabs = slabs.reshape((planes, 2, 2) + slabs.shape[1:])
         slabs = core_half(slabs, core, 2)
-        got = xor_swap(pick(slabs, 1 - y_at, 1), 4)
-        slabs = add_low(pick(slabs, y_at, 1), got).astype(jnp.bfloat16)
-        mine = plane_sum(slabs, plane, planes).astype(jnp.bfloat16)
-        return add_low(mine, xor_swap(mine, 1))
-
-    def x_then_y(slabs):
+        return pick(slabs, y_at, 1), xor_swap(pick(slabs, 1 - y_at, 1), 4)
+
+    def x_first(slabs):
         slabs = slabs.reshape((planes, 2, 2) + slabs.shape[1:])
         slabs = core_half(slabs, core, 2)
-        slabs = slabs.reshape(planes, 2, 2, slabs.shape[2] // 2, -1)
-        got = xor_swap(pick(slabs, 1 - x_at, 2), 1)
-        slabs = add_low(pick(slabs, x_at, 2), got).astype(jnp.bfloat16)
-        got = xor_swap(pick(slabs, 1 - y_at, 1), 4)
-        slabs = add_low(pick(slabs, y_at, 1), got).astype(jnp.bfloat16)
-        mine = plane_sum(slabs, plane, planes).astype(jnp.bfloat16)
-        other = xor_swap(mine, 1)
-        low_x = x_at == 0
-        return jnp.concatenate(
-            [jnp.where(low_x, mine, other), jnp.where(low_x, other, mine)], axis=0
-        ).astype(jnp.float32)
-
-    down_total = x_then_y(down_slabs)
-    up_total = y_then_x(up_slabs)
-    out_total = y_then_x(out_slabs)
-
-    back = attend_back(idx, live, queries, grad_ctx, pieces)
-    grad_q, kv_parts = back[0], back[1:]
-    sums = [add_low(kv_parts[2 * r], xor_swap(kv_parts[2 * r + 1], 2)) for r in range(3)]
-    grad_kv = (
-        sums[1]
-        + plane_shift(sums[0].astype(jnp.bfloat16), -1).astype(jnp.float32)
-        + plane_shift(sums[2].astype(jnp.bfloat16), 1).astype(jnp.float32)
-    ).astype(jnp.bfloat16)
+        size = slabs.shape[3] // 2
+
+        def side(at):
+            return lax.dynamic_slice_in_dim(slabs, at * size, size, 3)
+
+        return side(x_at), xor_swap(side(1 - x_at), 1)
+
+    down_pair = x_first(down_slabs)
+    up_pair = y_first(up_slabs)
+    out_pair = y_first(out_slabs)
+
+    grad_q, grad_kv = attend_back(idx, live, queries, grad_ctx, keys_values)
     wq_plain = jnp.pad(columns(w_query), ((0, 0), (0, WIN - WQ)))
-    grad_stretch = jnp.dot(grad_q, wq_plain.T, preferred_element_type=jnp.float32) + jnp.dot(
-        grad_kv, wkv_own.T, preferred_element_type=jnp.float32
-    )
-    sent = grad_stretch.astype(jnp.bfloat16).reshape(4, piece, width)
-    grad_tokens = grad_one + grad_stretch[:piece] + add_low(
-        xor_swap(sent[1], 1), xor_swap(sent[2], 4), xor_swap(sent[3], 5)
-    )
-
-    grad_wq = low_dot(stretch.T, grad_q)[:, :WQ]
-    grad_wkv = low_dot(stretch.T, grad_kv)
-    proj = jnp.concatenate([grad_wq, grad_wkv], axis=1).reshape(planes, 2, 2, share, 3 * WQ)
-    proj = core_half(proj, core, 2)
-    proj = plane_sum(proj, plane, planes).astype(jnp.bfloat16)
-    kept, given = pick(proj, y_at, 0), pick(proj, 1 - y_at, 0)
-    quarters = jnp.stack([kept, xor_swap(kept, 1), xor_swap(given, 4), xor_swap(given, 5)])
+    grad_attend, quarters, up_two, down_two, out_two = reduce_all(
+        grad_kv, grad_q, stretch, wq_plain, wkv_own, up_pair, out_pair, down_pair, planes
+    )
+    grad_tokens = grad_one + grad_attend
+
+    def joined(two):
+        return jnp.concatenate([two[0], two[1]], axis=1).astype(jnp.float32)
+
+    up_total, down_total, out_total = joined(up_two), joined(down_two), joined(out_two)
     quarters = [pick(quarters, g, 0) for g in order]
 
-    def whole(n):
-        return jnp.concatenate([q[:, n * WQ : (n + 1) * WQ] for q in quarters], axis=1).astype(
-            jnp.float32
-        )
+    def whole(at):
+        return jnp.concatenate([q[:, at : at + WQ] for q in quarters], axis=1).astype(jnp.float32)
 
     norm_row = out_total[share]
 
@@ -482,9 +905,9 @@
     return (
         output.astype(jnp.bfloat16),
         grad_tokens,
+        whole(2 * WQ),
         whole(0),
-        whole(1),
-        whole(2),
+        whole(WQ),
         out_total[:share],
         norm_grad(0),
         norm_grad(1),

time: 417 us -> 326 us (0.78)
  Pallas kernels: 57.7 us -> 189 us
  waiting for transfers between devices: 142 us -> 19 us
  starting transfers between devices: 114 us -> 13.1 us
  local copies, waits for them, and re-layouts: 19.5 us -> 34 us
  matrix products: 50.3 us -> 37.8 us
    pallas_call x0 -> x2, Pallas kernels: none -> 134 us  [the longest x1 94.4 us: reduce_all(): pl.pallas_call(functools.partial(reduce_kernel, planes, 0), out_shape=[sd...]
    ppermute x28 -> x0, starting transfers between devices: 87.4 us -> none  [plane_shift(): lax.ppermute(value, AXES, [(d, d + gap) for d in range(count) if 0 <= d +...]
    ppermute x28 -> x0, waiting for transfers between devices: 66.8 us -> none  [plane_shift(): lax.ppermute(value, AXES, [(d, d + gap) for d in range(count) if 0 <= d +...]
    ppermute x32 -> x12, waiting for transfers between devices: 74.9 us -> 19 us  [xor_swap(): return lax.ppermute(value, AXES, [(d, d ^ bits) for d in range(count)])]
    ppermute x32 -> x12, starting transfers between devices: 25.5 us -> 11.5 us  [xor_swap(): return lax.ppermute(value, AXES, [(d, d ^ bits) for d in range(count)])]
    dot_general x8 -> x4, matrix products: 24.1 us -> 13.9 us  [low_dot(): jnp.dot(a, b, preferred_element_type=jnp.float32).astype(jnp.bfloat16)]
    unnamed x87 -> x92, local copies, waits for them, and re-layouts: 4.05 us -> 13.6 us
    convert_element_type x4 -> x3, other arithmetic: 1.87 us -> 6.83 us  [core_half(): return add_low(pick(slabs, core, axis), got).astype(jnp.bfloat16)]
  transfers between devices with their start and end apart: 61 -> 13, of which waited for: 21 -> 5; matrix products, arithmetic and copies ran while one was open for 12% -> 11% of each run, Pallas kernels for 9% -> 24%
where the time goes in v2:
time: 326 us; the launch traced here: 320 us
  Pallas kernels  189 us (58%)
  matrix products  37.8 us (12%)
  local copies, waits for them, and re-layouts  34 us (10%)
  other arithmetic  25.1 us (8%)
  waiting for transfers between devices  19 us (6%)
  starting transfers between devices  13.1 us (4%)
    pallas_call x1, Pallas kernels, reduce_all(): pl.pallas_call(functools.partial(reduce_kernel, planes, 0), out_shape=[sd...  94.4 us
    pallas_call x1, Pallas kernels, gather_project(): pl.pallas_call(functools.partial(gather_kernel, planes), out_shape=[jax.S...  39.5 us
    pallas_call x1, Pallas kernels, attend_back(): pl.pallas_call(backward_kernel, out_shape=[jax.ShapeDtypeStruct((count, W...  38.5 us
    ppermute x12, waiting for transfers between devices, xor_swap(): return lax.ppermute(value, AXES, [(d, d ^ bits) for d in range(count)])  19 us
    pallas_call x1, Pallas kernels, attend(): pl.pallas_call(forward_kernel, out_shape=jax.ShapeDtypeStruct((count, WIN...  16.6 us
    dot_general x4, matrix products, low_dot(): jnp.dot(a, b, preferred_element_type=jnp.float32).astype(jnp.bfloat16)  13.9 us
    unnamed x92, local copies, waits for them, and re-layouts  13.6 us
    ppermute x12, starting transfers between devices, xor_swap(): return lax.ppermute(value, AXES, [(d, d ^ bits) for d in range(count)])  11.5 us
  transfers between devices with their start and end apart: 13, of which 5 were waited for; matrix products, arithmetic and copies ran while one was open for 11% of the time, Pallas kernels for 24%

profile of v2, /device:TPU:24, one launch (start us, length us, event | category | flops | bytes accessed | tf_op | source)
XLA Modules:
  0.0 319.5 jit_solution(9064398246694190151)
XLA Ops:
  4.5 2.4 broadcast_multiply_fusion
  8.0 39.5 %gather_project.1 = (bf16[12288,384]{1,0:T(8,128)(2,1)S(1)}, bf16[2048,256]{1,0:T(8,128)(2,1)S(1)}, bf16[2048,768]{1,0:T(8,128)(2,1)S(1)}) custom-call(bf16[512,768]{1,0:T(8,128)(2,1)S(1)} %copy-done.5, bf16[768,256]{1,0:T(8,128)(2,1)S(1)} %pad.25.wq_ref, bf16[768,384]{1,0:T(8,128)(2,1)S(1)} %pad_maximum_fusion.3.wkv_ref.refs_4_), custom_call_target="tpu_custom_call" | custom-call | flops 2013265920 | bytes 41943040 | tf_op jit(solution)/shard_map/gather_project/pallas_call | solution.py:354
  49.2 3.6 %copy-done.6 = bf16[12288,384]{1,0:T(8,128)(2,1)} copy-done((bf16[12288,384]{1,0:T(8,128)(2,1)}, bf16[12288,384]{1,0:T(8,128)(2,1)S(1)}, u32[]{:S(2)}) %copy-start.6) | copy-done | bytes 9437208
  53.8 3.7 %copy-done.7 = bf16[12288,384]{1,0:T(8,128)(2,1)S(1)} copy-done((bf16[12288,384]{1,0:T(8,128)(2,1)S(1)}, bf16[12288,384]{1,0:T(8,128)(2,1)}, u32[]{:S(2)}) %copy-start.7) | copy-done | bytes 9437208
  57.5 16.6 %attend.1 = bf16[2048,256]{1,0:T(8,128)(2,1)S(1)} custom-call(s32[256]{0:T(256)S(1)} %fusion.39.idx_ref, f32[32,512]{1,0:T(8,128)S(1)} %reshape.457.bias_ref, bf16[2048,256]{1,0:T(8,128)(2,1)S(1)} %get-tuple-element.22.q_ref, bf16[12288,384]{1,0:T(8,128)(2,1)S(1)} %copy-done.7), custom_call_target="tpu_custom_call" | custom-call | flops 6442450944 | bytes 9437184 | tf_op jit(solution)/shard_map/attend/pallas_call | solution.py:383
  80.1 4.2 %collective-permute-done.1 = bf16[512,256]{1,0:T(8,128)(2,1)S(1)} collective-permute-done((bf16[512,256]{1,0:T(8,128)(2,1)}, bf16[512,256]{1,0:T(8,128)(2,1)S(1)}, u32[]{:S(2)}, u32[]{:S(2)}) %collective-permute-start.1) | collective-permute-done | bytes 262176 | tf_op jit(solution)/shard_map/ppermute | solution.py:25
  84.4 5.0 %collective-permute-done.3 = bf16[512,256]{1,0:T(8,128)(2,1)S(1)} collective-permute-done((bf16[512,256]{1,0:T(8,128)(2,1)S(1)}, bf16[512,256]{1,0:T(8,128)(2,1)S(1)}, u32[]{:S(2)}, u32[]{:S(2)}) %collective-permute-start.3) | collective-permute-done | bytes 262176 | tf_op jit(solution)/shard_map/ppermute | solution.py:25
  90.2 2.4 fusion.60
  93.4 2.7 fusion.46
  96.1 3.9 %fusion.61 = (f32[512]{0:T(512)S(1)}, f32[512,768]{1,0:T(8,128)S(1)}) fusion(bf16[3072,768]{1,0:T(8,128)(2,1)S(1)} %bitcast.164, f32[512,3072]{1,0:T(8,128)S(1)} %fusion.46, f32[768]{0:T(1024)S(1)} %copy-done.37, f32[768]{0:T(1024)S(1)} %copy-done.30, f32[512]{0:T(512)S(1)} %add_rsqrt_fusion.1, f32[512,768]{1,0:T(8,128)S(1)} %get-tuple-element.111, ...), kind=kOutput, calls=%fused_computation.207 | convolution fusion | flops 2432433664 | bytes 14168064 | tf_op jit(solution)/shard_map/dot_general | solution.py:832
  102.2 4.1 %convolution_convert_fusion = bf16[3072,768]{1,0:T(8,128)(2,1)S(1)} fusion(f32[512,3072]{1,0:T(8,128)S(1)} %fusion.46, bf16[512,768]{1,0:T(8,128)(2,1)S(1)} %copy-done.14, f32[512,768]{1,0:T(8,128)S(1)} %get-tuple-element.113, f32[512]{0:T(512)S(1)} %broadcast_multiply_fusion.3, f32[512]{0:T(512)S(1)} %broadcast_multiply_fusion.4, f32[768]{0:T(1024)S(1)} %copy-done.29, ...), kind=kOutput, calls=%fused_computation.10 | convolution fusion | flops 2435973120 | bytes 13380608 | tf_op jit(solution)/shard_map/dot_general | solution.py:815
  106.3 8.6 %fusion.6 = bf16[512,3072]{1,0:T(8,128)(2,1)} fusion(f32[512,3072]{1,0:T(8,128)S(1)} %fusion.46, bf16[3072,768]{1,0:T(8,128)(2,1)S(1)} %bitcast.164, bf16[512,768]{1,0:T(8,128)(2,1)S(1)} %copy-done.14, f32[512,768]{1,0:T(8,128)S(1)} %get-tuple-element.113, f32[512]{0:T(512)S(1)} %broadcast_multiply_fusion.3, f32[512]{0:T(512)S(1)} %broadcast_multiply_fusion.4, ...), kind=kOutput, calls=%fused_computation.8 | convolution fusion | flops 2450915328 | bytes 16526336 | tf_op jit(solution)/shard_map/dot_general | solution.py:838
  114.9 6.3 %multiply_reduce_fusion = (bf16[768]{0:T(1024)(128)(2,1)S(1)}, f32[512]{0:T(512)S(1)}, f32[512]{0:T(512)S(1)}, bf16[768]{0:T(1024)(128)(2,1)S(1)}, f32[512,768]{1,0:T(8,128)}) fusion(f32[512,768]{1,0:T(8,128)S(1)} %get-tuple-element.111, f32[512]{0:T(512)S(1)} %add_rsqrt_fusion.1, f32[512]{0:T(512)S(1)} %broadcast_multiply_fusion.6, ...), kind=kOutput, calls=%fused_computation.50 | convolution fusion | flops 2422994432 | bytes 13394944 | tf_op jit(solution)/shard_map/dot_general | solution.py:841
  121.2 4.8 %convolution_convert_fusion.1 = bf16[768,3072]{1,0:T(8,128)(2,1)} fusion(bf16[512,3072]{1,0:T(8,128)(2,1)S(1)} %copy-done.38, f32[512,768]{1,0:T(8,128)S(1)} %get-tuple-element.111, f32[768]{0:T(1024)S(1)} %copy-done.37, f32[768]{0:T(1024)S(1)} %copy-done.30, f32[512]{0:T(512)S(1)} %add_rsqrt_fusion.1, f32[512]{0:T(512)S(1)} %broadcast_multiply_fusion.6), kind=kOutput, calls=%fused_computation.11 | convolution fusion | flops 2420244480 | bytes 9447424 | tf_op jit(solution)/shard_map/dot_general | solution.py:815
  128.2 2.0 subtract_multiply_fusion
  135.9 4.0 %convolution_convert_fusion.3 = bf16[512,1024]{1,0:T(8,128)(2,1)S(1)} fusion(f32[512,768]{1,0:T(8,128)S(1)} %subtract_multiply_fusion, bf16[192,768]{1,0:T(8,128)(2,1)S(1)} %copy-done.24, bf16[192,768]{1,0:T(8,128)(2,1)S(1)} %copy-done.26, bf16[192,768]{1,0:T(8,128)(2,1)S(1)} %copy-done.22, bf16[192,768]{1,0:T(8,128)(2,1)S(1)} %copy-done.20), kind=kOutput, calls=%fused_computation.58 | convolution fusion | flops 821952512 | bytes 3801088 | tf_op jit(solution)/shard_map/dot_general | solution.py:815
  142.9 6.3 %collective-permute-done.4 = bf16[512,256]{1,0:T(8,128)(2,1)} collective-permute-done((bf16[512,256]{1,0:T(8,128)(2,1)S(1)}, bf16[512,256]{1,0:T(8,128)(2,1)}, u32[]{:S(2)}, u32[]{:S(2)}) %collective-permute-start.4) | collective-permute-done | bytes 262176 | tf_op jit(solution)/shard_map/ppermute | solution.py:25
  150.6 1.8 pad.30.refs_3_
  154.5 3.3 %collective-permute-done.6 = bf16[512,256]{1,0:T(8,128)(2,1)} collective-permute-done((bf16[512,256]{1,0:T(8,128)(2,1)}, bf16[512,256]{1,0:T(8,128)(2,1)}, u32[]{:S(2)}, u32[]{:S(2)}) %collective-permute-start.6) | collective-permute-done | bytes 262176 | tf_op jit(solution)/shard_map/ppermute | solution.py:25
  157.8 2.3 pad_maximum_fusion.2.do_ref
  163.7 2.9 fusion.7
  168.5 2.6 fusion.8
  173.8 38.5 %attend_back.1 = (bf16[2048,256]{1,0:T(8,128)(2,1)}, bf16[12288,384]{1,0:T(8,128)(2,1)}) custom-call(s32[256]{0:T(256)} %copy-done.4, s32[256]{0:T(256)} %reshape.460.live_ref, bf16[2048,256]{1,0:T(8,128)(2,1)} %copy-done.8, bf16[2048,256]{1,0:T(8,128)(2,1)} %pad_maximum_fusion.2.do_ref, bf16[12288,384]{1,0:T(8,128)(2,1)} %copy-done.6), custom_call_target="tpu_custom_call" | custom-call | flops 16106127360 | bytes 18874368 | tf_op jit(solution)/shard_map/attend_back/pallas_call | solution.py:404
  214.1 94.4 %reduce_all.1 = (f32[512,768]{1,0:T(8,128)}, bf16[4,48,640]{2,1,0:T(8,128)(2,1)}, bf16[2,48,1536]{2,1,0:T(8,128)(2,1)}, bf16[2,192,384]{2,1,0:T(8,128)(2,1)}, bf16[2,64,384]{2,1,0:T(8,128)(2,1)}) custom-call(bf16[12288,384]{1,0:T(8,128)(2,1)} %get-tuple-element.24.refs_0_, bf16[2048,256]{1,0:T(8,128)(2,1)} %get-tuple-element.25.refs_1_, ...), custom_call_target="tpu_custom_call" | custom-call | flops 4026531840 | bytes 41943040 | tf_op jit(solution)/shard_map/reduce_all/pallas_call | solution.py:667
  (199 shorter events, 52.0 us)
Async XLA Ops:
  0.7 52.2 %collective-permute-start = (s32[16,3]{0,1:T(4,128)}, s32[16,3]{0,1:T(4,128)S(1)}, u32[]{:S(2)}, u32[]{:S(2)}) collective-permute-start(s32[16,3]{0,1:T(4,128)} %param.29), channel_id=1, source_target_pairs={{0,4},{2,6},{4,0},{6,2},{8,12},{10,14},{12,8},{14,10},{16,20},{18,... | collective-permute-start | bytes 584 | tf_op jit(solution)/shard_map/ppermute | solution.py:769
  7.1 40.4 %copy-start.3 = (bf16[768,384]{1,0:T(8,128)(2,1)}, bf16[768,384]{1,0:T(8,128)(2,1)S(1)}, u32[]{:S(2)}) copy-start(bf16[768,384]{1,0:T(8,128)(2,1)S(1)} %pad_maximum_fusion.3.wkv_ref.refs_4_) | copy-start | bytes 1769476
  52.9 21.2 %copy-start.8 = (bf16[2048,256]{1,0:T(8,128)(2,1)}, bf16[2048,256]{1,0:T(8,128)(2,1)S(1)}, u32[]{:S(2)}) copy-start(bf16[2048,256]{1,0:T(8,128)(2,1)S(1)} %get-tuple-element.22.q_ref) | copy-start | bytes 3145732
  53.8 20.3 %copy-start.4 = (s32[256]{0:T(256)}, s32[256]{0:T(256)S(1)}, u32[]{:S(2)}) copy-start(s32[256]{0:T(256)S(1)} %fusion.39.idx_ref) | copy-start | bytes 3076
  75.0 9.3 %collective-permute-start.1 = (bf16[512,256]{1,0:T(8,128)(2,1)}, bf16[512,256]{1,0:T(8,128)(2,1)S(1)}, u32[]{:S(2)}, u32[]{:S(2)}) collective-permute-start(bf16[512,256]{1,0:T(8,128)(2,1)} %get-tuple-element.76), channel_id=1, source_target_pairs={{0,1},{1,0},{2,3},{3,2},{4,5},{5,4},{6,7},{7,6},{8,9},{9,8},{10,11... | collective-permute-start | bytes 786440 | tf_op jit(solution)/shard_map/ppermute | solution.py:25
  75.5 8.9 %collective-permute-start.2 = (bf16[512,256]{1,0:T(8,128)(2,1)S(1)}, bf16[512,256]{1,0:T(8,128)(2,1)S(1)}, u32[]{:S(2)}, u32[]{:S(2)}) collective-permute-start(bf16[512,256]{1,0:T(8,128)(2,1)S(1)} %get-tuple-element.75), channel_id=1, source_target_pairs={{0,4},{1,5},{2,6},{3,7},{4,0},{5,1},{6,2},{7,3},{8,12},{9,13},{10,... | collective-permute-start | bytes 786440 | tf_op jit(solution)/shard_map/ppermute | solution.py:25
  77.0 12.4 %collective-permute-start.3 = (bf16[512,256]{1,0:T(8,128)(2,1)S(1)}, bf16[512,256]{1,0:T(8,128)(2,1)S(1)}, u32[]{:S(2)}, u32[]{:S(2)}) collective-permute-start(bf16[512,256]{1,0:T(8,128)(2,1)S(1)} %get-tuple-element.74), channel_id=1, source_target_pairs={{0,5},{1,4},{2,7},{3,6},{4,1},{5,0},{6,3},{7,2},{8,13},{9,12},{10,... | collective-permute-start | bytes 786440 | tf_op jit(solution)/shard_map/ppermute | solution.py:25
  80.0 12.5 %copy-start.19 = (bf16[192,768]{1,0:T(8,128)(2,1)}, bf16[192,768]{1,0:T(8,128)(2,1)S(1)}, u32[]{:S(2)}) copy-start(bf16[192,768]{1,0:T(8,128)(2,1)S(1)} %get-tuple-element.65) | copy-start | bytes 884740
  80.1 12.5 %copy-start.21 = (bf16[192,768]{1,0:T(8,128)(2,1)}, bf16[192,768]{1,0:T(8,128)(2,1)S(1)}, u32[]{:S(2)}) copy-start(bf16[192,768]{1,0:T(8,128)(2,1)S(1)} %get-tuple-element.66) | copy-start | bytes 884740
  80.1 12.5 %copy-start.23 = (bf16[192,768]{1,0:T(8,128)(2,1)}, bf16[192,768]{1,0:T(8,128)(2,1)S(1)}, u32[]{:S(2)}) copy-start(bf16[192,768]{1,0:T(8,128)(2,1)S(1)} %get-tuple-element.67) | copy-start | bytes 884740
  80.1 12.5 %copy-start.25 = (bf16[192,768]{1,0:T(8,128)(2,1)}, bf16[192,768]{1,0:T(8,128)(2,1)S(1)}, u32[]{:S(2)}) copy-start(bf16[192,768]{1,0:T(8,128)(2,1)S(1)} %get-tuple-element.68) | copy-start | bytes 884740
  106.2 19.8 %copy-start.11 = (bf16[3072,768]{1,0:T(8,128)(2,1)}, bf16[3072,768]{1,0:T(8,128)(2,1)S(1)}, u32[]{:S(2)}) copy-start(bf16[3072,768]{1,0:T(8,128)(2,1)S(1)} %convolution_convert_fusion) | copy-start | bytes 14155780
  114.9 6.3 %copy-start.38 = (bf16[512,3072]{1,0:T(8,128)(2,1)S(1)}, bf16[512,3072]{1,0:T(8,128)(2,1)}, u32[]{:S(2)}) copy-start(bf16[512,3072]{1,0:T(8,128)(2,1)} %fusion.6) | copy-start | bytes 9437188
  127.6 36.0 %collective-permute-start.11 = (bf16[4,2,192,768]{3,2,1,0:T(8,128)(2,1)}, bf16[4,2,192,768]{3,2,1,0:T(8,128)(2,1)}, u32[]{:S(2)}, u32[]{:S(2)}) collective-permute-start(bf16[4,2,192,768]{3,2,1,0:T(8,128)(2,1)} %dynamic-slice_bitcast_fusion), channel_id=1, source_target_pairs={{0,2},{1,3},{2,0},{3,1},{4,6},{5,7},{6,4},{7,5},{8,10},{9,11},{10,... | collective-permute-start | bytes 7077896 | tf_op jit(solution)/shard_map/ppermute | solution.py:25
  130.2 5.7 %copy-start.9 = (f32[512,768]{1,0:T(8,128)}, f32[512,768]{1,0:T(8,128)S(1)}, u32[]{:S(2)}) copy-start(f32[512,768]{1,0:T(8,128)S(1)} %subtract_multiply_fusion) | copy-start | bytes 4718596
  132.5 27.5 %collective-permute-start.9 = (bf16[4,2,64,768]{3,2,1,0:T(8,128)(2,1)}, bf16[4,2,64,768]{3,2,1,0:T(8,128)(2,1)}, u32[]{:S(2)}, u32[]{:S(2)}) collective-permute-start(bf16[4,2,64,768]{3,2,1,0:T(8,128)(2,1)} %fusion.28), channel_id=1, source_target_pairs={{0,2},{1,3},{2,0},{3,1},{4,6},{5,7},{6,4},{7,5},{8,10},{9,11},{10,... | collective-permute-start | bytes 2359304 | tf_op jit(solution)/shard_map/ppermute | solution.py:25
  135.4 33.1 %collective-permute-start.7 = (bf16[4,2,48,3072]{3,2,0,1:T(8,128)(2,1)}, bf16[4,2,48,3072]{3,2,0,1:T(8,128)(2,1)}, u32[]{:S(2)}, u32[]{:S(2)}) collective-permute-start(bf16[4,2,48,3072]{3,2,0,1:T(8,128)(2,1)} %bitcast.150), channel_id=1, source_target_pairs={{0,2},{1,3},{2,0},{3,1},{4,6},{5,7},{6,4},{7,5},{8,10},{9,11},{10,... | collective-permute-start | bytes 7077896 | tf_op jit(solution)/shard_map/ppermute | solution.py:25
  140.8 8.3 %collective-permute-start.4 = (bf16[512,256]{1,0:T(8,128)(2,1)S(1)}, bf16[512,256]{1,0:T(8,128)(2,1)}, u32[]{:S(2)}, u32[]{:S(2)}) collective-permute-start(bf16[512,256]{1,0:T(8,128)(2,1)S(1)} %get-tuple-element.72), channel_id=1, source_target_pairs={{0,1},{1,0},{2,3},{3,2},{4,5},{5,4},{6,7},{7,6},{8,9},{9,8},{10,11... | collective-permute-start | bytes 786440 | tf_op jit(solution)/shard_map/ppermute | solution.py:25
  142.3 12.1 %collective-permute-start.5 = (bf16[512,256]{1,0:T(8,128)(2,1)}, bf16[512,256]{1,0:T(8,128)(2,1)}, u32[]{:S(2)}, u32[]{:S(2)}) collective-permute-start(bf16[512,256]{1,0:T(8,128)(2,1)} %get-tuple-element.71), channel_id=1, source_target_pairs={{0,4},{1,5},{2,6},{3,7},{4,0},{5,1},{6,2},{7,3},{8,12},{9,13},{10,... | collective-permute-start | bytes 786440 | tf_op jit(solution)/shard_map/ppermute | solution.py:25
  149.2 8.6 %collective-permute-start.6 = (bf16[512,256]{1,0:T(8,128)(2,1)}, bf16[512,256]{1,0:T(8,128)(2,1)}, u32[]{:S(2)}, u32[]{:S(2)}) collective-permute-start(bf16[512,256]{1,0:T(8,128)(2,1)} %get-tuple-element.70), channel_id=1, source_target_pairs={{0,5},{1,4},{2,7},{3,6},{4,1},{5,0},{6,3},{7,2},{8,13},{9,12},{10,... | collective-permute-start | bytes 786440 | tf_op jit(solution)/shard_map/ppermute | solution.py:25
  154.5 5.6 %copy-start.13 = (bf16[16,16,768]{2,1,0:T(8,128)(2,1)S(1)}, bf16[16,16,768]{2,1,0:T(8,128)(2,1)}, u32[]{:S(2)}) copy-start(bf16[16,16,768]{2,1,0:T(8,128)(2,1)} %copy-done.12) | copy-start | bytes 1179652
  162.2 50.1 %collective-permute-start.10 = (bf16[4,64,768]{2,1,0:T(8,128)(2,1)S(1)}, bf16[4,64,768]{2,1,0:T(8,128)(2,1)S(1)}, u32[]{:S(2)}, u32[]{:S(2)}) collective-permute-start(bf16[4,64,768]{2,1,0:T(8,128)(2,1)S(1)} %get-tuple-element.77), channel_id=1, source_target_pairs={{0,4},{1,5},{2,6},{3,7},{4,0},{5,1},{6,2},{7,3},{8,12},{9,13},{10,... | collective-permute-start | bytes 1179656 | tf_op jit(solution)/shard_map/ppermute | solution.py:25
  168.0 44.3 %collective-permute-start.12 = (bf16[4,2,192,384]{3,2,1,0:T(8,128)(2,1)S(1)}, bf16[4,2,192,384]{3,2,1,0:T(8,128)(2,1)S(1)}, u32[]{:S(2)}, u32[]{:S(2)}) collective-permute-start(bf16[4,2,192,384]{3,2,1,0:T(8,128)(2,1)S(1)} %get-tuple-element.56), channel_id=1, source_target_pairs={{0,1},{1,0},{2,3},{3,2},{4,5},{5,4},{6,7},{7,6},{8,9},{9,8},{10,11... | collective-permute-start | bytes 3538952 | tf_op jit(solution)/shard_map/ppermute | solution.py:25
  172.3 40.1 %collective-permute-start.8 = (bf16[4,48,3072]{2,1,0:T(8,128)(2,1)S(1)}, bf16[4,48,3072]{2,1,0:T(8,128)(2,1)S(1)}, u32[]{:S(2)}, u32[]{:S(2)}) collective-permute-start(bf16[4,48,3072]{2,1,0:T(8,128)(2,1)S(1)} %get-tuple-element.58), channel_id=1, source_target_pairs={{0,4},{1,5},{2,6},{3,7},{4,0},{5,1},{6,2},{7,3},{8,12},{9,13},{10,... | collective-permute-start | bytes 3538952 | tf_op jit(solution)/shard_map/ppermute | solution.py:25
  (34 other events, 88.3 us)
